TPU v7x, 32 devices: a whole 2x2x4 slice. The times are simulated.
32 devices in a mesh: row: 16 (over z, y, x), col: 2 (over core).
Axes of the slice: x: 2, y: 2, z: 4, core: 2. Of those that a mesh axis runs over, the one named last changes fastest.
Arguments:
- matrix: float32 [2, 16, 4, 2, 256, 256], P(None, 'row', None, 'col'), as said below
- keep_mask: int32 [2, 16, 4, 2], P(None, 'row', None, 'col'), may hold values 0 or 1
Outputs:
- factored: float32 [2, 16, 4, 2, 256, 256], P(None, 'row', None, 'col')
Inputs may be any that keep to these rules, and one draw needn't show every extreme that they name: `matrix`: tiles whose row and column index are equal are symmetric, and the symmetric completion of the kept tiles in the window's leading two tile rows and columns is positive definite, so that both panel steps meet positive definite diagonal tiles.
All inputs are finite; a program needn't handle non-finite values. No bound on the sum of `keep_mask` on one device may be relied on, other than what follows from the above.
Results may differ from a plain program's by a relative error of at most 0.0001.
Values sent between devices are 32-bit elements; how exact they have to be, the bound alone decides.
No kernel may reach another device: no remote copies, remote signals or barrier semaphores. Data moves between devices by JAX's collectives and lax.ppermute only.
A program may use at most 64 MiB of HBM per device.

v0:
```python
import jax
import jax.numpy as jnp
from jax import lax
from jax.sharding import PartitionSpec as P

HALF_BAND = 256


def broadcast(shard, axis, root):
    mine = lax.axis_index(axis) == root
    return lax.psum(jnp.where(mine, shard, jnp.zeros_like(shard)), axis)


def right_solve(factor_diag, blocks):
    block_count, tile_edge = (blocks.shape[0], blocks.shape[1])
    stacked = jnp.transpose(blocks, (2, 0, 1)).reshape(tile_edge, block_count * tile_edge)
    solved = lax.linalg.triangular_solve(factor_diag, stacked, left_side=True, lower=True)
    return jnp.transpose(solved.reshape(tile_edge, block_count, tile_edge), (1, 2, 0))


def local(matrix, keep_mask):
    blocks = matrix[:, 0, :, 0]
    kept_marks = keep_mask[:, 0, :, 0]
    row_count, pair_count, tile_edge = (blocks.shape[0], blocks.shape[1], blocks.shape[-1])
    row_devices = lax.axis_size("row")
    row_place = lax.axis_index("row")
    col_place = lax.axis_index("col")
    tile_row = jnp.arange(row_count, dtype=jnp.int32)[:, None] * row_devices + row_place
    tile_col = 2 * jnp.arange(pair_count, dtype=jnp.int32)[None, :] + col_place
    kept_tile = (
        ((kept_marks == 1) | (tile_row == tile_col))
        & (tile_row >= tile_col)
        & (tile_row - tile_col <= HALF_BAND)
    )
    blocks = jnp.where(kept_tile[:, :, None, None], blocks, 0.0)
    lower_part = tile_row >= tile_col
    identity = jnp.eye(tile_edge, dtype=jnp.float32)
    row_index = tile_row[:, 0][:, None, None]
    for panel_step in range(2):
        diag_block = broadcast(blocks[0, 0], "row", panel_step)
        factor_diag = jnp.linalg.cholesky(jnp.where(col_place == panel_step, diag_block, identity))
        solved = right_solve(factor_diag, blocks[:, 0])
        factor_panel_col = jnp.where(
            row_index > panel_step,
            solved,
            jnp.where(row_index == panel_step, factor_diag[None], 0.0),
        )
        factor_panel_col = broadcast(factor_panel_col, "col", panel_step)
        unused = jnp.zeros((tile_edge, tile_edge), jnp.float32)
        leading = [unused for source in range(panel_step + 1)]
        trailing = [
            broadcast(factor_panel_col[0], "row", source)
            for source in range(panel_step + 1, 2 * pair_count)
        ]
        factor_column_set = jnp.stack(leading + trailing)
        column = jnp.where(col_place == panel_step, factor_panel_col, blocks[:, 0])
        blocks = blocks.at[:, 0].set(column)
        paired = factor_column_set.reshape(pair_count, 2, tile_edge, tile_edge)
        my_columns = jnp.where(col_place == 0, paired[:, 0], paired[:, 1])
        product = jnp.einsum(
            "tab,scb->tsac",
            factor_panel_col,
            my_columns,
            precision=lax.Precision.HIGHEST,
            preferred_element_type=jnp.float32,
        )
        selected = (lower_part & (tile_col > panel_step))[:, 0:pair_count, None, None]
        updated = blocks - jnp.where(selected, product, 0.0)
        blocks = jnp.concatenate([blocks[:, :0], updated, blocks[:, pair_count:]], axis=1)
    return blocks[:, None, :, None]


def solution(mesh):
    return jax.shard_map(
        local,
        mesh=mesh,
        in_specs=(P(None, "row", None, "col", None, None), P(None, "row", None, "col")),
        out_specs=P(None, "row", None, "col", None, None),
        check_vma=False,
    )
```

profile of v0, /device:TPU:25, one launch (start us, length us, event | category | flops | bytes accessed | tf_op | source)
XLA Modules:
  0.0 715.5 jit_solution(1143109675651483619)
XLA Ops:
  6.6 2.9 copy.20
  9.5 1.9 bitcast_select_fusion.2
  12.3 1.0 copy.23
  13.8 103.4 %all-reduce.10.cloned.1.call-done = f32[256,256]{0,1:T(8,128)} async-done(((f32[256,256]{0,1:T(8,128)}), f32[256,256]{0,1:T(8,128)}) %all-reduce.10.cloned.1.call-update) | async-done | bytes 262160 | tf_op jit(solution)/shard_map/psum | solution.py:11
  117.3 0.8 copy.21
  118.1 1.0 fusion.24
  119.8 11.7 %cholesky.130 = f32[128,128]{1,0:T(8,128)S(1)} custom-call(f32[128,128]{1,0:T(8,128)S(1)} %cholesky.194), custom_call_target="Cholesky" | custom-call | tf_op jit(solution)/shard_map/jit(cholesky)/cholesky | solution.py:41
  132.1 9.8 %custom-call.13 = f32[1,128,128]{1,2,0:T(8,128)S(1)} custom-call(f32[1,128,128]{2,1,0:T(8,128)S(1)} %get-tuple-element.112), custom_call_target="InvertDiagBlocksLowerTriangular" | custom-call | tf_op jit(solution)/shard_map/jit(cholesky)/cholesky | solution.py:41
  141.9 1.0 constant_dynamic-update-slice_fusion.16
  143.0 1.1 convolution_subtract_fusion.3
  144.1 11.7 %cholesky.147 = f32[128,128]{1,0:T(8,128)S(1)} custom-call(f32[128,128]{1,0:T(8,128)S(1)} %convolution_subtract_fusion.3), custom_call_target="Cholesky" | custom-call | tf_op jit(solution)/shard_map/jit(cholesky)/cholesky | solution.py:41
  155.8 1.4 compare_reduce_fusion.3
  159.3 1.7 fusion.27
  161.0 1.2 broadcast.416
  162.3 5.2 while.6
  163.7 1.3 bitcast_dynamic-update-slice_fusion.4
  166.2 1.3 bitcast_dynamic-update-slice_fusion.4
  168.1 20.5 %custom-call.14 = f32[2,128,128]{1,2,0:T(8,128)S(1)} custom-call(f32[2,128,128]{2,1,0:T(8,128)} %copy-done.13), custom_call_target="InvertDiagBlocksLowerTriangular" | custom-call | tf_op jit(solution)/shard_map/triangular_solve/custom-call.0 | solution.py:17
  190.2 1.0 copy.24
  191.1 1.2 copy.25
  192.4 0.8 copy.26
  193.2 1.9 fusion.14
  195.2 22.6 %all-reduce.12.cloned.1.call-done = f32[2,256,256]{1,2,0:T(8,128)} async-done(((f32[2,256,256]{1,2,0:T(8,128)}), f32[2,256,256]{1,2,0:T(8,128)}) %all-reduce.12.cloned.1.call-update) | async-done | bytes 524304 | tf_op jit(solution)/shard_map/psum | solution.py:11
  217.8 2.3 slice_select_fusion.8
  220.2 0.7 broadcast_dynamic-update-slice_fusion.1
  221.0 126.6 %all-reduce.20.cloned.1.call-done = (f32[1,256,256]{1,2,0:T(8,128)}, f32[1,256,256]{1,2,0:T(8,128)}, f32[1,256,256]{1,2,0:T(8,128)}, f32[1,256,256]{1,2,0:T(8,12...) async-done(((f32[1,256,256]{1,2,0:T(8,128)}, f32[1,256,256]{1,2,0:T(8,128)}, f32[1,256,256]{1,2,0:T(8,128)}, f32[1,256,256]{1,2,0:T(8,128)}, ...) | async-done | bytes 1835024 | tf_op jit(solution)/shard_map/psum | solution.py:11
  347.6 1.7 constant_dynamic-update-slice_fusion.6
  349.3 1.7 constant_dynamic-update-slice_fusion.5
  351.0 1.7 constant_dynamic-update-slice_fusion.4
  352.7 1.7 constant_dynamic-update-slice_fusion.3
  354.3 0.7 constant_dynamic-update-slice_fusion.2
  355.1 0.7 constant_dynamic-update-slice_fusion.1
  355.8 0.7 constant_dynamic-update-slice_fusion
  356.5 3.0 fusion.44
  359.5 1.6 copy.53
  361.1 2.5 copy.54
  363.6 3.3 fusion.2
  366.9 1.3 copy-done
  369.2 1.1 fusion.43
  370.6 102.9 %all-reduce.14.cloned.1.call-done = f32[256,256]{0,1:T(8,128)} async-done(((f32[256,256]{0,1:T(8,128)}), f32[256,256]{0,1:T(8,128)}) %all-reduce.14.cloned.1.call-update) | async-done | bytes 262160 | tf_op jit(solution)/shard_map/psum | solution.py:11
  473.4 1.0 convert_select_fusion
  474.6 1.0 fusion.23
  475.6 11.7 %cholesky.164 = f32[128,128]{1,0:T(8,128)S(1)} custom-call(f32[128,128]{1,0:T(8,128)S(1)} %cholesky.197), custom_call_target="Cholesky" | custom-call | tf_op jit(solution)/shard_map/jit(cholesky)/cholesky | solution.py:41
  487.3 9.8 %custom-call.15 = f32[1,128,128]{1,2,0:T(8,128)S(1)} custom-call(f32[1,128,128]{2,1,0:T(8,128)S(1)} %get-tuple-element.108), custom_call_target="InvertDiagBlocksLowerTriangular" | custom-call | tf_op jit(solution)/shard_map/jit(cholesky)/cholesky | solution.py:41
  497.6 11.7 %cholesky.181 = f32[128,128]{1,0:T(8,128)S(1)} custom-call(f32[128,128]{1,0:T(8,128)S(1)} %convolution_subtract_fusion.2), custom_call_target="Cholesky" | custom-call | tf_op jit(solution)/shard_map/jit(cholesky)/cholesky | solution.py:41
  512.3 4.6 while.7
  513.2 1.5 bitcast_dynamic-update-slice_fusion.5
  515.4 1.5 bitcast_dynamic-update-slice_fusion.5
  516.9 19.7 %custom-call.16 = f32[2,128,128]{1,2,0:T(8,128)S(1)} custom-call(f32[2,128,128]{2,1,0:T(8,128)S(1)} %get-tuple-element.46), custom_call_target="InvertDiagBlocksLowerTriangular" | custom-call | tf_op jit(solution)/shard_map/triangular_solve/custom-call.0 | solution.py:17
  538.6 0.9 fusion.13
  539.6 19.7 %all-reduce.16.cloned.1.call-done = f32[2,256,256]{1,2,0:T(8,128)} async-done(((f32[2,256,256]{1,2,0:T(8,128)}), f32[2,256,256]{1,2,0:T(8,128)}) %all-reduce.16.cloned.1.call-update) | async-done | bytes 524304 | tf_op jit(solution)/shard_map/psum | solution.py:11
  559.3 2.2 slice_select_fusion.2
  561.6 0.8 broadcast_dynamic-update-slice_fusion
  562.5 123.0 %all-reduce.18.cloned.1.call-done = (f32[1,256,256]{1,2,0:T(8,128)}, f32[1,256,256]{1,2,0:T(8,128)}, f32[1,256,256]{1,2,0:T(8,128)}, f32[1,256,256]{1,2,0:T(8,12...) async-done(((f32[1,256,256]{1,2,0:T(8,128)}, f32[1,256,256]{1,2,0:T(8,128)}, f32[1,256,256]{1,2,0:T(8,128)}, f32[1,256,256]{1,2,0:T(8,128)}, f32[1,256,256]{1,2,0:T(8,128)}, ...) | async-done | bytes 1572880 | tf_op jit(solution)/shard_map/psum | solution.py:11
  685.5 1.7 constant_dynamic-update-slice_fusion.12
  687.2 1.7 constant_dynamic-update-slice_fusion.11
  688.9 1.7 constant_dynamic-update-slice_fusion.10
  690.6 1.7 constant_dynamic-update-slice_fusion.9
  692.9 0.7 constant_dynamic-update-slice_fusion.7
  693.7 3.0 fusion.42
  696.7 1.6 copy.56
  698.2 2.5 copy.57
  700.8 4.6 fusion.1
  705.3 2.9 copy.42
  (95 shorter events, 16.0 us)
Async XLA Ops:
  6.5 110.7 %all-reduce.10.cloned.1.call-start = ((), (), s32[]{:S(2)}) async-start(), calls=%async_computation | async-start | bytes 524288 | tf_op jit(solution)/shard_map/psum | solution.py:11
  6.5 2.9 copy-start.14
  12.2 205.7 %all-reduce.12.cloned.1.call-start = ((), (), s32[]{:S(2)}) async-start(), calls=%async_computation.1 | async-start | bytes 1048576 | tf_op jit(solution)/shard_map/psum | solution.py:11
  117.3 71.4 %copy-start.4 = (f32[256,2,256]{0,2,1:T(8,128)S(1)}, f32[256,2,256]{0,2,1:T(8,128)}, u32[]{:S(2)}) copy-start(f32[256,2,256]{0,2,1:T(8,128)} %copy.23) | copy-start | bytes 1572868
  119.1 0.7 copy-start.7
  157.2 2.1 copy-start.5
  167.5 0.6 copy-start.13
  189.7 2.7 copy-start.6
  195.1 152.4 %all-reduce.20.cloned.1.call-start = ((), (), s32[]{:S(2)}) async-start(), calls=%async_computation.5 | async-start | bytes 3670016 | tf_op jit(solution)/shard_map/psum | solution.py:11
  217.8 3.1 copy-start.2
  220.1 253.3 %all-reduce.14.cloned.1.call-start = ((), (), s32[]{:S(2)}) async-start(), calls=%async_computation.2 | async-start | bytes 524288 | tf_op jit(solution)/shard_map/psum | solution.py:11
  347.6 6.8 copy-start.10
  347.6 7.5 %copy-start.9 = (f32[1,256,256]{1,2,0:T(8,128)S(1)}, f32[1,256,256]{1,2,0:T(8,128)}, u32[]{:S(2)}) copy-start(f32[1,256,256]{1,2,0:T(8,128)} %get-tuple-element.74) | copy-start | bytes 786436
  347.6 8.2 %copy-start.8 = (f32[1,256,256]{1,2,0:T(8,128)S(1)}, f32[1,256,256]{1,2,0:T(8,128)}, u32[]{:S(2)}) copy-start(f32[1,256,256]{1,2,0:T(8,128)} %get-tuple-element.75) | copy-start | bytes 786436
  366.9 1.3 copy-start
  369.0 190.4 %all-reduce.16.cloned.1.call-start = ((), (), s32[]{:S(2)}) async-start(), calls=%async_computation.3 | async-start | bytes 1048576 | tf_op jit(solution)/shard_map/psum | solution.py:11
  370.6 141.7 %copy-start.15 = (s32[2,2]{1,0:T(2,128)S(1)}, s32[2,2]{1,0:T(2,128)}, u32[]{:S(2)}) copy-start(s32[2,2]{1,0:T(2,128)} %get-tuple-element.288) | copy-start | bytes 52
  539.5 22.9 %copy-start.1 = (f32[2,4,256,256]{2,3,1,0:T(8,128)S(1)}, f32[2,4,256,256]{2,3,1,0:T(8,128)}, u32[]{:S(2)}) copy-start(f32[2,4,256,256]{2,3,1,0:T(8,128)} %copy-done) | copy-start | bytes 6291460
  539.6 145.9 %all-reduce.18.cloned.1.call-start = ((), (), s32[]{:S(2)}) async-start(), calls=%async_computation.4 | async-start | bytes 3145728 | tf_op jit(solution)/shard_map/psum | solution.py:11
  559.3 3.1 copy-start.3
  685.5 6.7 copy-start.12
  685.5 7.5 %copy-start.11 = (f32[1,256,256]{1,2,0:T(8,128)S(1)}, f32[1,256,256]{1,2,0:T(8,128)}, u32[]{:S(2)}) copy-start(f32[1,256,256]{1,2,0:T(8,128)} %get-tuple-element.68) | copy-start | bytes 786436
Sparse Core Ops, SparseCore 0:
  12.6 104.6 all-reduce.9
  195.3 22.5 all-reduce.11
  224.3 123.2 all-reduce.19
  369.1 104.3 all-reduce.13
  539.7 19.6 all-reduce.15
  566.6 118.8 all-reduce.17
where the time goes:
time: 728 us; the launch traced here: 716 us
  waiting for transfers between devices  498 us (68%)
  other arithmetic  127 us (17%)
  local copies, waits for them, and re-layouts  58.8 us (8%)
  between operations  17.1 us (2%)
  matrix products  13.3 us (2%)
    psum x6, waiting for transfers between devices, broadcast(): return lax.psum(jnp.where(mine, shard, jnp.zeros_like(shard)), axis)  498 us
    another operation x14, other arithmetic, local(): jnp.linalg.cholesky(jnp.where(col_place == panel_step, diag_block, identi...  70.6 us
    another operation x7, other arithmetic, right_solve(): lax.linalg.triangular_solve(factor_diag, stacked, left_side=True, lower=T...  42.5 us
    unnamed x50, local copies, waits for them, and re-layouts  31 us
  transfers between devices with their start and end apart: 6, of which 6 were waited for; matrix products, arithmetic and copies ran while one was open for 1% of the time, Pallas kernels for 0%

commit v1 on v0

v1 whole, which is shorter than its diff:
```python
import jax
import jax.numpy as jnp
from jax import lax
from jax.experimental import pallas as pl
from jax.experimental.pallas import tpu as pltpu
from jax.sharding import PartitionSpec as P

HALF_BAND = 256
F32 = jnp.float32
VMEM = pl.BlockSpec(memory_space=pltpu.VMEM)
SMEM = pl.BlockSpec(memory_space=pltpu.SMEM)


def dot(a, b, da, db):
    return lax.dot_general(
        a,
        b,
        (((da,), (db,)), ((), ())),
        precision=lax.Precision.HIGHEST,
        preferred_element_type=F32,
    )


def lanes(x, j):
    return jnp.broadcast_to(x[:, j : j + 1], x.shape)


def rows(x, r):
    return jnp.broadcast_to(x[r : r + 1, :], x.shape)


def factor128(a):
    n = a.shape[0] // 8
    sub = lax.broadcasted_iota(jnp.int32, (8, 128), 0)
    lane = lax.broadcasted_iota(jnp.int32, (8, 128), 1)
    left = [a[8 * i : 8 * i + 8, :] for i in range(n)]
    right = [jnp.where(lane == sub + 8 * i, 1.0, 0.0).astype(F32) for i in range(n)]
    upper, inverse = [], []
    for k in range(n):
        column = [lanes(left[k], 8 * k + s) for s in range(8)]
        pivot = {(r, s): rows(column[s], r) for s in range(8) for r in range(s, 8)}
        low, scale = {}, []
        for s in range(8):
            scale.append(lax.rsqrt(pivot[s, s]))
            for r in range(s + 1, 8):
                low[r, s] = pivot[r, s] * scale[s]
            for t in range(s + 1, 8):
                for r in range(t, 8):
                    pivot[r, t] = pivot[r, t] - low[r, s] * low[t, s]
        u, v = [], []
        for s in range(8):
            x, y = rows(left[k], s), rows(right[k], s)
            for t in range(s):
                x, y = x - low[s, t] * u[t], y - low[s, t] * v[t]
            u.append(x * scale[s])
            v.append(y * scale[s])
        x, y = u[7], v[7]
        for s in range(6, -1, -1):
            x, y = jnp.where(sub == s, u[s], x), jnp.where(sub == s, v[s], y)
        upper.append(x)
        inverse.append(y)
        if k + 1 < n:
            solved = []
            for s in range(8):
                x = lanes(left[k + 1], 8 * k + s)
                for t in range(s):
                    x = x - low[s, t] * solved[t]
                solved.append(x * scale[s])
            for s in range(8):
                left[k + 1] = left[k + 1] - solved[s] * u[s]
                right[k + 1] = right[k + 1] - solved[s] * v[s]
        if k + 2 < n:
            for s in range(7, -1, -1):
                for t in range(s + 1, 8):
                    u[s], v[s] = u[s] - low[t, s] * u[t], v[s] - low[t, s] * v[t]
                u[s], v[s] = u[s] * scale[s], v[s] * scale[s]
            for i in range(k + 2, n):
                column = [lanes(left[i], 8 * k + s) for s in range(8)]
                for s in range(8):
                    left[i] = left[i] - column[s] * u[s]
                    right[i] = right[i] - column[s] * v[s]
    return jnp.concatenate(upper, 0), jnp.concatenate(inverse, 0)


def inverse_factor(a_ref, out_ref):
    h = a_ref.shape[0] // 2
    _, inv0 = factor128(a_ref[:h, :h])
    upper = dot(inv0, a_ref[:h, h:], 1, 0)
    _, inv1 = factor128(a_ref[h:, h:] - dot(upper, upper, 0, 0))
    out_ref[:h, :h] = inv0
    out_ref[:h, h:] = jnp.zeros((h, h), F32)
    out_ref[h:, :h] = -dot(inv1, dot(upper, inv0, 0, 0), 1, 0)
    out_ref[h:, h:] = inv1


def first_kernel(place_ref, own_ref, other_ref, inv_ref, tile_ref):
    tile_ref[...] = jnp.where(place_ref[1] == 0, own_ref[...], other_ref[...])
    inverse_factor(tile_ref, inv_ref)


def second_kernel(place_ref, own_ref, other_ref, inv0_ref, low_ref, inv1_ref, tile_ref):
    first = place_ref[1] == 0
    below = jnp.where(first, own_ref[...], other_ref[...])
    low = dot(below, inv0_ref[...], 1, 1)
    low_ref[...] = low
    tile_ref[...] = jnp.where(first, other_ref[...], own_ref[...]) - dot(low, low, 1, 1)
    inverse_factor(tile_ref, inv1_ref)


def solve(left, right, inv0, low, inv1):
    first = dot(left, inv0, 1, 1)
    return first, dot(right - dot(first, low, 1, 1), inv1, 1, 1)


def last_kernel(
    place_ref, keep_ref, tiles_ref, own_ref, other_ref, near_ref, far_ref,
    inv0_ref, low_ref, inv1_ref, out_ref, panel_ref,
):
    p, q = place_ref[0], place_ref[1]
    row_devices = place_ref[2]
    edge = tiles_ref.shape[-1]
    inv0, low, inv1 = inv0_ref[...], low_ref[...], inv1_ref[...]
    lower = lax.broadcasted_iota(jnp.int32, (edge, edge), 0) >= lax.broadcasted_iota(
        jnp.int32, (edge, edge), 1
    )
    pairs = tiles_ref.shape[1]
    base = lax.rem(p, 8) // 2
    for s in range(1, pairs):
        slot = jnp.bitwise_xor(base, s)
        slot = jnp.where(q == 0, slot, (slot % 2) * 2 + slot // 2)
        source = slot % 2
        left = jnp.where(slot < 2, near_ref[source, 0], far_ref[source, 0])
        right = jnp.where(slot < 2, near_ref[source, 1], far_ref[source, 1])
        panel_ref[s, 0], panel_ref[s, 1] = solve(left, right, inv0, low, inv1)
    for t in range(tiles_ref.shape[0]):
        i = t * row_devices + p
        left = jnp.where(q == 0, own_ref[t], other_ref[t])
        right = jnp.where(q == 0, other_ref[t], own_ref[t])
        first, second = solve(left, right, inv0, low, inv1)
        first = jnp.where((i > 0) | lower, first, 0.0)
        second = jnp.where((i > 1) | ((i == 1) & lower), second, 0.0)
        out_ref[t, 0] = jnp.where(q == 0, first, second)
        for s in range(1, pairs):
            tile = jnp.where(keep_ref[t, s] == 1, tiles_ref[t, s], 0.0)
            out_ref[t, s] = tile

            @pl.when(2 * s + q <= i)
            def _():
                out_ref[t, s] = tile - (
                    dot(first, panel_ref[s, 0], 1, 1) + dot(second, panel_ref[s, 1], 1, 1)
                )


def call(kernel, name, outs, specs, scratch, flops, *args):
    return pl.pallas_call(
        kernel,
        out_shape=outs,
        in_specs=specs,
        out_specs=jax.tree.map(lambda _: VMEM, outs),
        scratch_shapes=scratch,
        name=name,
        cost_estimate=pl.CostEstimate(flops=flops, bytes_accessed=1 << 20, transcendentals=0),
        compiler_params=pltpu.CompilerParams(vmem_limit_bytes=48 << 20),
    )(*args)


def local(matrix, keep_mask):
    tiles = matrix[:, 0, :, 0]
    row_count, pair_count, edge = tiles.shape[0], tiles.shape[1], tiles.shape[-1]
    n = lax.axis_size("row")
    p, q = lax.axis_index("row"), lax.axis_index("col")
    tile_row = jnp.arange(row_count, dtype=jnp.int32)[:, None] * n + p
    tile_col = 2 * jnp.arange(pair_count, dtype=jnp.int32)[None, :] + q
    keep = (
        ((keep_mask[:, 0, :, 0] == 1) | (tile_row == tile_col))
        & (tile_row >= tile_col)
        & (tile_row - tile_col <= HALF_BAND)
    ).astype(jnp.int32)
    place = jnp.stack([p, q, jnp.int32(n)]).astype(jnp.int32)

    def send(x, pairs):
        return lax.ppermute(x, ("row", "col"), [(2 * a + b, 2 * c + d) for a, b, c, d in pairs])

    own = jnp.where((keep[:, 0] == 1)[:, None, None], tiles[:, 0], 0.0)
    other = send(own, [(i, c, i, 1 - c) for i in range(n) for c in range(2)])
    mine = own[0]

    bits = [1, 2]
    high = n // 2
    while high > 2:
        bits.append(high)
        high //= 2
    lead, next_lead = mine, mine
    r = send(next_lead, [(1, c, 0, c) for c in range(2)])
    next_lead = jnp.where(p == 0, r, next_lead)
    have = [0]
    for bit in bits:
        r = send(lead, [(i, 0, i + bit, 0) for i in have])
        lead = jnp.where(jnp.bitwise_and(p, bit) > 0, r, lead)
        if bit > 1:
            r = send(next_lead, [(i, c, i + bit, c) for i in have for c in range(2)])
            next_lead = jnp.where(jnp.bitwise_and(p, bit) > 0, r, next_lead)
        have = have + [i + bit for i in have]
    lead_other = send(lead, [(i, 0, i, 1) for i in range(n)])
    next_other = send(next_lead, [(i, c, i, 1 - c) for i in range(n) for c in range(2)])

    pair = jnp.where(q == 0, jnp.stack([mine, other[0]]), jnp.stack([other[0], mine]))
    size = 8
    while size < n:
        r = send(pair, [(i, i % 2, i + size, i % 2) for i in range(size) if i % 8 > 1])
        pair = jnp.where((p >= size) & (p < 2 * size), r, pair)
        size *= 2
    r = send(pair, [(i, i % 2, i ^ 1, i % 2) for i in range(n) if i % 8 > 1])
    pair = jnp.where(jnp.bitwise_and(p, 1) == q, pair, r)
    flips = (2, 4)
    r = send(pair, [(i, c, i ^ flips[c], c) for i in range(n) for c in range(2)])
    near = jnp.stack([pair, r])
    far = send(near, [(i, c, i ^ flips[1 - c], c) for i in range(n) for c in range(2)])

    tile = jax.ShapeDtypeStruct((edge, edge), F32)
    room = [pltpu.VMEM((edge, edge), F32)]
    inv0 = call(
        first_kernel, "first", tile, [SMEM, VMEM, VMEM], room, 10**10, place, lead, lead_other
    )
    low, inv1 = call(
        second_kernel, "second", [tile, tile], [SMEM, VMEM, VMEM, VMEM], room, 10**10,
        place, next_lead, next_other, inv0,
    )
    out = call(
        last_kernel, "last", jax.ShapeDtypeStruct(tiles.shape, F32),
        [SMEM, SMEM] + [VMEM] * 8, [pltpu.VMEM((pair_count, 2, edge, edge), F32)], 10**10,
        place, keep, tiles, own, other, near, far, inv0, low, inv1,
    )
    return out[:, None, :, None]


def solution(mesh):
    return jax.shard_map(
        local,
        mesh=mesh,
        in_specs=(P(None, "row", None, "col", None, None), P(None, "row", None, "col")),
        out_specs=P(None, "row", None, "col", None, None),
        check_vma=False,
    )
```

time: 728 us -> 87 us (0.12); the launches traced: 716 us -> 86.6 us
  waiting for transfers between devices: 498 us -> 13.7 us
  other arithmetic: 127 us -> 3.68 us
  local copies, waits for them, and re-layouts: 58.8 us -> 1.79 us
  starting transfers between devices: 0.42 us -> 34.1 us
  Pallas kernels: 0 us -> 33 us
  between operations: 17.1 us -> 0.29 us
  matrix products: 13.3 us -> 0 us
    psum x6 -> x0, waiting for transfers between devices: 498 us -> none  [broadcast(): return lax.psum(jnp.where(mine, shard, jnp.zeros_like(shard)), axis)]
    another operation x21 -> x2, other arithmetic: 113 us -> 0.15 us  [the longest x1 0.08 us: local(): place = jnp.stack([p, q, jnp.int32(n)]).astype(jnp.int32)]
    ppermute x0 -> x15, starting transfers between devices: none -> 34.1 us  [send(): lax.ppermute(x, ('row', 'col'), [(2 * a + b, 2 * c + d) for a, b, c, d in...]
    pallas_call x0 -> x3, Pallas kernels: none -> 33 us  [call(): pl.pallas_call(kernel, out_shape=outs, in_specs=specs, out_specs=jax.tree...]
    unnamed x50 -> x3, local copies, waits for them, and re-layouts: 31 us -> 1.73 us
    ppermute x0 -> x15, waiting for transfers between devices: none -> 13.7 us  [send(): lax.ppermute(x, ('row', 'col'), [(2 * a + b, 2 * c + d) for a, b, c, d in...]
    another operation x23 -> x0, local copies, waits for them, and re-layouts: 13.2 us -> none  [the longest x17 11.7 us: right_solve(): lax.linalg.triangular_solve(factor_diag, stacked, left_side=True, lower=T...]
    select_n x9 -> x11, other arithmetic: 11.6 us -> 2.64 us  [the longest x1 1.12 us: local(): pair = jnp.where((p >= size) & (p < 2 * size), r, pair)]
  transfers between devices with their start and end apart: 6 -> 15, of which waited for: 6 -> 3; matrix products, arithmetic and copies ran while one was open for 1% -> 3% of each run, Pallas kernels for 0% -> 25%
where the time goes in v1:
time: 87 us; the launch traced here: 86.6 us
  starting transfers between devices  34.1 us (39%)
  Pallas kernels  33 us (38%)
  waiting for transfers between devices  13.7 us (16%)
  other arithmetic  3.68 us (4%)
  local copies, waits for them, and re-layouts  1.79 us (2%)
    ppermute x15, starting transfers between devices, send(): lax.ppermute(x, ('row', 'col'), [(2 * a + b, 2 * c + d) for a, b, c, d in...  34.1 us
    pallas_call x3, Pallas kernels, call(): pl.pallas_call(kernel, out_shape=outs, in_specs=specs, out_specs=jax.tree...  33 us
    ppermute x15, waiting for transfers between devices, send(): lax.ppermute(x, ('row', 'col'), [(2 * a + b, 2 * c + d) for a, b, c, d in...  13.7 us
  transfers between devices with their start and end apart: 15, of which 3 were waited for; matrix products, arithmetic and copies ran while one was open for 3% of the time, Pallas kernels for 25%

profile of v1, /device:TPU:25, one launch (start us, length us, event | category | flops | bytes accessed | tf_op | source)
XLA Modules:
  0.0 86.6 jit_solution(225911785888422344)
XLA Ops:
  0.0 0.7 broadcast_compare_fusion
  0.7 0.1 fusion.3.keep_ref
  0.8 0.1 compare_reduce_fusion
  0.9 1.7 %copy.10 = f32[2,1,4,1,256,256]{5,4,0,2,3,1:T(8,128)S(1)} copy(f32[2,1,4,1,256,256]{5,4,3,2,1,0:T(8,128)} %param.2) | data formatting | bytes 4194304 | tf_op args[0]
  2.6 0.1 fusion.own_ref
  2.7 0.7 collective-permute-start
  3.5 0.7 collective-permute-start.10
  4.2 0.7 collective-permute-start.5
  4.9 0.1 collective-permute-done.other_ref
  5.1 1.5 %collective-permute-start.1 = (f32[2,256,256]{2,1,0:T(8,128)S(1)}, f32[2,256,256]{2,1,0:T(8,128)}, u32[]{:S(2)}, u32[]{:S(2)}) collective-permute-start(f32[2,256,256]{2,1,0:T(8,128)S(1)} %maximum_select_fusion), channel_id=1, source_target_pairs={{4,20},{7,23},{8,24},{11,27},{12,28},{15,31}} | collective-permute-start | bytes 1572872 | tf_op jit(solution)/shard_map/ppermute | solution.py:182
  6.5 0.0 collective-permute-done.10
  6.5 0.0 collective-permute-done.5
  6.6 0.1 broadcast_select_fusion.2
  6.6 0.7 collective-permute-start.11
  7.3 0.7 collective-permute-start.6
  8.0 0.0 collective-permute-done.11
  8.0 0.7 collective-permute-start.12
  8.7 0.0 collective-permute-done.1
  8.7 1.1 %broadcast_select_fusion = f32[2,256,256]{2,1,0:T(8,128)S(1)} fusion(f32[2,256,256]{2,1,0:T(8,128)} %collective-permute-done.1, pred[]{:T(512)S(6)} %and.30, f32[1,256,256]{2,1,0:T(8,128)S(1)} %get-tuple-element.12, f32[1,256,256]{2,1,0:T(8,128)S(1)} %slice.19, pred[]{:T(512)S(6)} %eq.46), kind=kLoop, calls=%fused_computation.5 | loop fusion | flops 524288 | bytes 1572866 | tf_op jit(solution)/shard_map/jit(_where)/select_n | solution.py:211
  9.9 1.3 %collective-permute-start.2 = (f32[2,256,256]{2,1,0:T(8,128)S(1)}, f32[2,256,256]{2,1,0:T(8,128)}, u32[]{:S(2)}, u32[]{:S(2)}) collective-permute-start(f32[2,256,256]{2,1,0:T(8,128)S(1)} %broadcast_select_fusion), channel_id=1, source_target_pairs={{4,6},{7,5},{8,10},{11,9},{12,14},{15,13},{20,22},{23,21},{24,26},... | collective-permute-start | bytes 1572872 | tf_op jit(solution)/shard_map/ppermute | solution.py:182
  11.2 0.0 collective-permute-done.6
  11.2 0.7 collective-permute-start.7
  11.9 0.0 collective-permute-done.12
  12.0 1.3 %collective-permute-start.13 = (f32[256,256]{1,0:T(8,128)S(1)}, f32[256,256]{1,0:T(8,128)S(1)}, u32[]{:S(2)}, u32[]{:S(2)}) collective-permute-start(f32[256,256]{1,0:T(8,128)S(1)} %broadcast_select_fusion.6), channel_id=1, source_target_pairs={{0,8},{1,9},{2,10},{3,11},{4,12},{5,13},{6,14},{7,15},{16,24},{17,... | collective-permute-start | bytes 786440 | tf_op jit(solution)/shard_map/ppermute | solution.py:182
  13.3 0.0 collective-permute-done.7
  13.3 0.7 collective-permute-start.8
  14.0 12.3 %collective-permute-done.2 = f32[2,256,256]{2,1,0:T(8,128)} collective-permute-done((f32[2,256,256]{2,1,0:T(8,128)S(1)}, f32[2,256,256]{2,1,0:T(8,128)}, u32[]{:S(2)}, u32[]{:S(2)}) %collective-permute-start.2) | collective-permute-done | bytes 524320 | tf_op jit(solution)/shard_map/ppermute | solution.py:182
  26.3 1.1 %broadcast_select_fusion.1 = f32[2,256,256]{2,1,0:T(8,128)S(1)} fusion(f32[2,256,256]{2,1,0:T(8,128)S(1)} %broadcast_select_fusion, f32[2,256,256]{2,1,0:T(8,128)} %collective-permute-done.2, pred[]{:T(512)S(6)} %eq.45), kind=kLoop, calls=%fused_computation.6 | loop fusion | flops 131072 | bytes 1572865 | tf_op jit(solution)/shard_map/jit(_where)/select_n | solution.py:214
  27.4 1.9 %collective-permute-start.3 = (f32[2,256,256]{2,1,0:T(8,128)S(1)}, f32[2,256,256]{2,1,0:T(8,128)S(1)}, u32[]{:S(2)}, u32[]{:S(2)}) collective-permute-start(f32[2,256,256]{2,1,0:T(8,128)S(1)} %broadcast_select_fusion.1), channel_id=1, source_target_pairs={{0,4},{1,9},{2,6},{3,11},{4,0},{5,13},{6,2},{7,15},{8,12},{9,1},{1... | collective-permute-start | bytes 1572872 | tf_op jit(solution)/shard_map/ppermute | solution.py:182
  29.3 0.1 pad_add_fusion.place_ref
  29.3 0.0 collective-permute-done.8
  29.4 1.3 %collective-permute-start.9 = (f32[256,256]{1,0:T(8,128)S(1)}, f32[256,256]{1,0:T(8,128)S(1)}, u32[]{:S(2)}, u32[]{:S(2)}) collective-permute-start(f32[256,256]{1,0:T(8,128)S(1)} %broadcast_select_fusion.9.own_ref), channel_id=1, source_target_pairs={{0,1},{2,3},{4,5},{6,7},{8,9},{10,11},{12,13},{14,15},{16,17},{18,... | collective-permute-start | bytes 786440 | tf_op jit(solution)/shard_map/ppermute | solution.py:182
  30.7 1.3 %collective-permute-done.13 = f32[256,256]{1,0:T(8,128)S(1)} collective-permute-done((f32[256,256]{1,0:T(8,128)S(1)}, f32[256,256]{1,0:T(8,128)S(1)}, u32[]{:S(2)}, u32[]{:S(2)}) %collective-permute-start.13) | collective-permute-done | bytes 262176 | tf_op jit(solution)/shard_map/ppermute | solution.py:182
  32.0 11.8 %collective-permute-start.14 = (f32[256,256]{1,0:T(8,128)S(1)}, f32[256,256]{1,0:T(8,128)S(1)}, u32[]{:S(2)}, u32[]{:S(2)}) collective-permute-start(f32[256,256]{1,0:T(8,128)S(1)} %broadcast_select_fusion.8.own_ref), channel_id=1, source_target_pairs={{0,1},{1,0},{2,3},{3,2},{4,5},{5,4},{6,7},{7,6},{8,9},{9,8},{10,11... | collective-permute-start | bytes 786440 | tf_op jit(solution)/shard_map/ppermute | solution.py:182
  43.8 0.0 collective-permute-done.3
  43.8 0.1 pad_maximum_fusion.near_ref
  43.9 9.6 %collective-permute-start.4 = (f32[2,2,256,256]{3,2,1,0:T(8,128)S(1)}, f32[2,2,256,256]{3,2,1,0:T(8,128)S(1)}, u32[]{:S(2)}, u32[]{:S(2)}) collective-permute-start(f32[2,2,256,256]{3,2,1,0:T(8,128)S(1)} %pad_maximum_fusion.near_ref), channel_id=1, source_target_pairs={{0,8},{1,5},{2,10},{3,7},{4,12},{5,1},{6,14},{7,3},{8,0},{9,13},{1... | collective-permute-start | bytes 3145736 | tf_op jit(solution)/shard_map/ppermute | solution.py:182
  53.5 0.0 collective-permute-done.9.other_ref
  53.5 10.1 %first.1.inv0_ref = f32[256,256]{1,0:T(8,128)S(1)} custom-call(s32[3]{0:T(128)S(1)} %pad_add_fusion.place_ref, f32[256,256]{1,0:T(8,128)S(1)} %broadcast_select_fusion.9.own_ref, f32[256,256]{1,0:T(8,128)S(1)} %collective-permute-done.9.other_ref), custom_call_target="tpu_custom_call" | custom-call | flops 10000000000 | bytes 1048576 | tf_op jit(solution)/shard_map/first/pallas_call | solution.py:155
  63.7 0.0 copy-start
  63.7 0.0 collective-permute-done.14.other_ref
  63.7 11.4 %second.1 = (f32[256,256]{1,0:T(8,128)S(1)}, f32[256,256]{1,0:T(8,128)S(1)}) custom-call(s32[3]{0:T(128)S(1)} %pad_add_fusion.place_ref, f32[256,256]{1,0:T(8,128)S(1)} %broadcast_select_fusion.8.own_ref, f32[256,256]{1,0:T(8,128)S(1)} %collective-permute-done.14.other_ref, f32[256,256]{1,0:T(8,128)S(1)} %first.1.inv0_ref), custom_call_target="tpu_custom_call" | custom-call | flops 10000000000 | bytes 1048576 | tf_op jit(solution)/shard_map/second/pallas_call | solution.py:155
  75.1 0.0 collective-permute-done.4.far_ref
  75.1 0.0 copy-done
  75.1 11.5 %last.1 = f32[2,4,256,256]{3,2,1,0:T(8,128)} custom-call(s32[3]{0:T(128)S(1)} %pad_add_fusion.place_ref, s32[2,4]{1,0:T(2,128)S(1)} %fusion.3.keep_ref, f32[2,4,256,256]{3,2,1,0:T(8,128)S(1)} %bitcast.27, f32[2,256,256]{2,1,0:T(8,128)S(1)} %fusion.own_ref, f32[2,256,256]{2,1,0:T(8,128)S(1)} %collective-permute-done.other_ref, ...), custom_call_target="tpu_custom_call" | custom-call | flops 10000000000 | bytes 1048576 | tf_op jit(solution)/shard_map/last/pallas_call | solution.py:155
  (11 shorter events, 0.3 us)
Async XLA Ops:
  2.7 2.3 %collective-permute-start = (f32[2,256,256]{2,1,0:T(8,128)S(1)}, f32[2,256,256]{2,1,0:T(8,128)S(1)}, u32[]{:S(2)}, u32[]{:S(2)}) collective-permute-start(f32[2,256,256]{2,1,0:T(8,128)S(1)} %fusion.own_ref), channel_id=1, source_target_pairs={{0,1},{1,0},{2,3},{3,2},{4,5},{5,4},{6,7},{7,6},{8,9},{9,8},{10,11... | collective-permute-start | bytes 1572872 | tf_op jit(solution)/shard_map/ppermute | solution.py:182
  3.5 3.0 %collective-permute-start.10 = (f32[256,256]{1,0:T(8,128)S(1)}, f32[256,256]{1,0:T(8,128)S(1)}, u32[]{:S(2)}, u32[]{:S(2)}) collective-permute-start(f32[256,256]{1,0:T(8,128)S(1)} %get-tuple-element.11), channel_id=1, source_target_pairs={{2,0},{3,1}} | collective-permute-start | bytes 786440 | tf_op jit(solution)/shard_map/ppermute | solution.py:182
  4.2 2.4 %collective-permute-start.5 = (f32[256,256]{1,0:T(8,128)S(1)}, f32[256,256]{1,0:T(8,128)S(1)}, u32[]{:S(2)}, u32[]{:S(2)}) collective-permute-start(f32[256,256]{1,0:T(8,128)S(1)} %get-tuple-element.11), channel_id=1, source_target_pairs={{0,2}} | collective-permute-start | bytes 786440 | tf_op jit(solution)/shard_map/ppermute | solution.py:182
  5.1 3.6 %collective-permute-start.1 = (f32[2,256,256]{2,1,0:T(8,128)S(1)}, f32[2,256,256]{2,1,0:T(8,128)}, u32[]{:S(2)}, u32[]{:S(2)}) collective-permute-start(f32[2,256,256]{2,1,0:T(8,128)S(1)} %maximum_select_fusion), channel_id=1, source_target_pairs={{4,20},{7,23},{8,24},{11,27},{12,28},{15,31}} | collective-permute-start | bytes 1572872 | tf_op jit(solution)/shard_map/ppermute | solution.py:182
  6.6 1.4 %collective-permute-start.11 = (f32[256,256]{1,0:T(8,128)S(1)}, f32[256,256]{1,0:T(8,128)S(1)}, u32[]{:S(2)}, u32[]{:S(2)}) collective-permute-start(f32[256,256]{1,0:T(8,128)S(1)} %get-tuple-element.9), channel_id=1, source_target_pairs={{0,4},{1,5},{2,6},{3,7}} | collective-permute-start | bytes 786440 | tf_op jit(solution)/shard_map/ppermute | solution.py:182
  7.3 3.9 %collective-permute-start.6 = (f32[256,256]{1,0:T(8,128)S(1)}, f32[256,256]{1,0:T(8,128)S(1)}, u32[]{:S(2)}, u32[]{:S(2)}) collective-permute-start(f32[256,256]{1,0:T(8,128)S(1)} %get-tuple-element.10), channel_id=1, source_target_pairs={{0,4},{2,6}} | collective-permute-start | bytes 786440 | tf_op jit(solution)/shard_map/ppermute | solution.py:182
  8.0 3.9 %collective-permute-start.12 = (f32[256,256]{1,0:T(8,128)S(1)}, f32[256,256]{1,0:T(8,128)S(1)}, u32[]{:S(2)}, u32[]{:S(2)}) collective-permute-start(f32[256,256]{1,0:T(8,128)S(1)} %broadcast_select_fusion.4), channel_id=1, source_target_pairs={{0,16},{1,17},{2,18},{3,19},{4,20},{5,21},{6,22},{7,23}} | collective-permute-start | bytes 786440 | tf_op jit(solution)/shard_map/ppermute | solution.py:182
  9.9 16.4 %collective-permute-start.2 = (f32[2,256,256]{2,1,0:T(8,128)S(1)}, f32[2,256,256]{2,1,0:T(8,128)}, u32[]{:S(2)}, u32[]{:S(2)}) collective-permute-start(f32[2,256,256]{2,1,0:T(8,128)S(1)} %broadcast_select_fusion), channel_id=1, source_target_pairs={{4,6},{7,5},{8,10},{11,9},{12,14},{15,13},{20,22},{23,21},{24,26},... | collective-permute-start | bytes 1572872 | tf_op jit(solution)/shard_map/ppermute | solution.py:182
  11.2 2.1 %collective-permute-start.7 = (f32[256,256]{1,0:T(8,128)S(1)}, f32[256,256]{1,0:T(8,128)S(1)}, u32[]{:S(2)}, u32[]{:S(2)}) collective-permute-start(f32[256,256]{1,0:T(8,128)S(1)} %broadcast_select_fusion.5), channel_id=1, source_target_pairs={{0,16},{2,18},{4,20},{6,22}} | collective-permute-start | bytes 786440 | tf_op jit(solution)/shard_map/ppermute | solution.py:182
  12.0 20.0 %collective-permute-start.13 = (f32[256,256]{1,0:T(8,128)S(1)}, f32[256,256]{1,0:T(8,128)S(1)}, u32[]{:S(2)}, u32[]{:S(2)}) collective-permute-start(f32[256,256]{1,0:T(8,128)S(1)} %broadcast_select_fusion.6), channel_id=1, source_target_pairs={{0,8},{1,9},{2,10},{3,11},{4,12},{5,13},{6,14},{7,15},{16,24},{17,... | collective-permute-start | bytes 786440 | tf_op jit(solution)/shard_map/ppermute | solution.py:182
  13.3 16.0 %collective-permute-start.8 = (f32[256,256]{1,0:T(8,128)S(1)}, f32[256,256]{1,0:T(8,128)S(1)}, u32[]{:S(2)}, u32[]{:S(2)}) collective-permute-start(f32[256,256]{1,0:T(8,128)S(1)} %broadcast_select_fusion.7), channel_id=1, source_target_pairs={{0,8},{2,10},{4,12},{6,14},{16,24},{18,26},{20,28},{22,30}} | collective-permute-start | bytes 786440 | tf_op jit(solution)/shard_map/ppermute | solution.py:182
  27.4 16.4 %collective-permute-start.3 = (f32[2,256,256]{2,1,0:T(8,128)S(1)}, f32[2,256,256]{2,1,0:T(8,128)S(1)}, u32[]{:S(2)}, u32[]{:S(2)}) collective-permute-start(f32[2,256,256]{2,1,0:T(8,128)S(1)} %broadcast_select_fusion.1), channel_id=1, source_target_pairs={{0,4},{1,9},{2,6},{3,11},{4,0},{5,13},{6,2},{7,15},{8,12},{9,1},{1... | collective-permute-start | bytes 1572872 | tf_op jit(solution)/shard_map/ppermute | solution.py:182
  29.4 24.2 %collective-permute-start.9 = (f32[256,256]{1,0:T(8,128)S(1)}, f32[256,256]{1,0:T(8,128)S(1)}, u32[]{:S(2)}, u32[]{:S(2)}) collective-permute-start(f32[256,256]{1,0:T(8,128)S(1)} %broadcast_select_fusion.9.own_ref), channel_id=1, source_target_pairs={{0,1},{2,3},{4,5},{6,7},{8,9},{10,11},{12,13},{14,15},{16,17},{18,... | collective-permute-start | bytes 786440 | tf_op jit(solution)/shard_map/ppermute | solution.py:182
  32.0 31.7 %collective-permute-start.14 = (f32[256,256]{1,0:T(8,128)S(1)}, f32[256,256]{1,0:T(8,128)S(1)}, u32[]{:S(2)}, u32[]{:S(2)}) collective-permute-start(f32[256,256]{1,0:T(8,128)S(1)} %broadcast_select_fusion.8.own_ref), channel_id=1, source_target_pairs={{0,1},{1,0},{2,3},{3,2},{4,5},{5,4},{6,7},{7,6},{8,9},{9,8},{10,11... | collective-permute-start | bytes 786440 | tf_op jit(solution)/shard_map/ppermute | solution.py:182
  43.9 31.2 %collective-permute-start.4 = (f32[2,2,256,256]{3,2,1,0:T(8,128)S(1)}, f32[2,2,256,256]{3,2,1,0:T(8,128)S(1)}, u32[]{:S(2)}, u32[]{:S(2)}) collective-permute-start(f32[2,2,256,256]{3,2,1,0:T(8,128)S(1)} %pad_maximum_fusion.near_ref), channel_id=1, source_target_pairs={{0,8},{1,5},{2,10},{3,7},{4,12},{5,1},{6,14},{7,3},{8,0},{9,13},{1... | collective-permute-start | bytes 3145736 | tf_op jit(solution)/shard_map/ppermute | solution.py:182
  63.7 11.4 %copy-start = (f32[2,1,4,1,256,256]{5,4,3,2,1,0:T(8,128)S(1)}, f32[2,1,4,1,256,256]{5,4,3,2,1,0:T(8,128)}, u32[]{:S(2)}) copy-start(f32[2,1,4,1,256,256]{5,4,3,2,1,0:T(8,128)} %param.2) | copy-start | bytes 6291460

commit v2 on v1

--- a/solution.py
+++ b/solution.py
@@ -113,7 +113,7 @@
 
 
 def last_kernel(
-    place_ref, keep_ref, tiles_ref, own_ref, other_ref, near_ref, far_ref,
+    place_ref, keep_ref, tiles_ref, own_ref, other_ref, at_ref, a_ref, b_ref, c_ref,
     inv0_ref, low_ref, inv1_ref, out_ref, panel_ref,
 ):
     p, q = place_ref[0], place_ref[1]
@@ -125,13 +125,16 @@
     )
     pairs = tiles_ref.shape[1]
     base = lax.rem(p, 8) // 2
-    for s in range(1, pairs):
-        slot = jnp.bitwise_xor(base, s)
-        slot = jnp.where(q == 0, slot, (slot % 2) * 2 + slot // 2)
-        source = slot % 2
-        left = jnp.where(slot < 2, near_ref[source, 0], far_ref[source, 0])
-        right = jnp.where(slot < 2, near_ref[source, 1], far_ref[source, 1])
-        panel_ref[s, 0], panel_ref[s, 1] = solve(left, right, inv0, low, inv1)
+    for here, ref in enumerate((at_ref, a_ref, b_ref, c_ref)):
+        flip = jnp.where(q == 0, here, (here % 2) * 2 + here // 2)
+        slot = jnp.bitwise_xor(base, flip)
+
+        @pl.when(slot > 0)
+        def _():
+            left = jnp.where(q == 0, ref[0], ref[1])
+            right = jnp.where(q == 0, ref[1], ref[0])
+            panel_ref[slot, 0], panel_ref[slot, 1] = solve(left, right, inv0, low, inv1)
+
     for t in range(tiles_ref.shape[0]):
         i = t * row_devices + p
         left = jnp.where(q == 0, own_ref[t], other_ref[t])
@@ -185,51 +188,56 @@
     other = send(own, [(i, c, i, 1 - c) for i in range(n) for c in range(2)])
     mine = own[0]
 
-    bits = [1, 2]
-    high = n // 2
-    while high > 2:
-        bits.append(high)
-        high //= 2
+    high = []
+    while 8 << len(high) < n:
+        high.append(8 << len(high))
     lead, next_lead = mine, mine
     r = send(next_lead, [(1, c, 0, c) for c in range(2)])
     next_lead = jnp.where(p == 0, r, next_lead)
-    have = [0]
-    for bit in bits:
+    have, next_have = [0], [0, 1]
+    for bit in high + [1, 2, 4]:
         r = send(lead, [(i, 0, i + bit, 0) for i in have])
         lead = jnp.where(jnp.bitwise_and(p, bit) > 0, r, lead)
-        if bit > 1:
-            r = send(next_lead, [(i, c, i + bit, c) for i in have for c in range(2)])
+        have = have + [i + bit for i in have]
+        if bit != 1:
+            r = send(next_lead, [(i, c, i + bit, c) for i in next_have for c in range(2)])
             next_lead = jnp.where(jnp.bitwise_and(p, bit) > 0, r, next_lead)
-        have = have + [i + bit for i in have]
+            next_have = next_have + [i + bit for i in next_have]
     lead_other = send(lead, [(i, 0, i, 1) for i in range(n)])
     next_other = send(next_lead, [(i, c, i, 1 - c) for i in range(n) for c in range(2)])
 
-    pair = jnp.where(q == 0, jnp.stack([mine, other[0]]), jnp.stack([other[0], mine]))
-    size = 8
-    while size < n:
-        r = send(pair, [(i, i % 2, i + size, i % 2) for i in range(size) if i % 8 > 1])
-        pair = jnp.where((p >= size) & (p < 2 * size), r, pair)
-        size *= 2
-    r = send(pair, [(i, i % 2, i ^ 1, i % 2) for i in range(n) if i % 8 > 1])
-    pair = jnp.where(jnp.bitwise_and(p, 1) == q, pair, r)
+    mine_here = mine
+    for size in high:
+        r = send(mine_here, [(i, c, i + size, c) for i in range(size) if i % 8 > 1 for c in range(2)])
+        mine_here = jnp.where((p >= size) & (p < 2 * size), r, mine_here)
+    sources = [i for i in range(n) if i % 8 > 1]
+    r1 = send(
+        mine_here,
+        [(i, i % 2, i ^ 1, i % 2) for i in sources] + [(i, 1 - i % 2, i, i % 2) for i in sources],
+    )
+    r2 = send(mine_here, [(i, 1 - i % 2, i ^ 1, i % 2) for i in sources])
+    home = jnp.bitwise_and(p, 1) == q
+    at = jnp.stack([jnp.where(home, mine_here, r1), jnp.where(home, r1, r2)])
     flips = (2, 4)
-    r = send(pair, [(i, c, i ^ flips[c], c) for i in range(n) for c in range(2)])
-    near = jnp.stack([pair, r])
-    far = send(near, [(i, c, i ^ flips[1 - c], c) for i in range(n) for c in range(2)])
+    ra = send(at, [(i, c, i ^ flips[c], c) for i in range(n) for c in range(2)])
+    rb = send(at, [(i, c, i ^ flips[1 - c], c) for i in range(n) for c in range(2)])
+    lead, at = lax.optimization_barrier((lead, at))
 
     tile = jax.ShapeDtypeStruct((edge, edge), F32)
     room = [pltpu.VMEM((edge, edge), F32)]
     inv0 = call(
         first_kernel, "first", tile, [SMEM, VMEM, VMEM], room, 10**10, place, lead, lead_other
     )
+    ra, inv0 = lax.optimization_barrier((ra, inv0))
+    rc = send(ra, [(i, c, i ^ flips[1 - c], c) for i in range(n) for c in range(2)])
     low, inv1 = call(
         second_kernel, "second", [tile, tile], [SMEM, VMEM, VMEM, VMEM], room, 10**10,
         place, next_lead, next_other, inv0,
     )
     out = call(
         last_kernel, "last", jax.ShapeDtypeStruct(tiles.shape, F32),
-        [SMEM, SMEM] + [VMEM] * 8, [pltpu.VMEM((pair_count, 2, edge, edge), F32)], 10**10,
-        place, keep, tiles, own, other, near, far, inv0, low, inv1,
+        [SMEM, SMEM] + [VMEM] * 10, [pltpu.VMEM((pair_count, 2, edge, edge), F32)], 10**10,
+        place, keep, tiles, own, other, at, ra, rb, rc, inv0, low, inv1,
     )
     return out[:, None, :, None]
 

time: 87 us -> 80.5 us (0.925)
  starting transfers between devices: 34.1 us -> 26 us
  other arithmetic: 3.68 us -> 1.45 us
  waiting for transfers between devices: 13.7 us -> 15.9 us
  Pallas kernels: 33 us -> 34.5 us
    ppermute x15 -> x17, starting transfers between devices: 34.1 us -> 26 us  [send(): lax.ppermute(x, ('row', 'col'), [(2 * a + b, 2 * c + d) for a, b, c, d in...]
    select_n x3 -> x0, other arithmetic: 2.27 us -> none  [the longest x1 1.12 us: local(): pair = jnp.where((p >= size) & (p < 2 * size), r, pair)]
    ppermute x15 -> x17, waiting for transfers between devices: 13.7 us -> 15.9 us  [send(): lax.ppermute(x, ('row', 'col'), [(2 * a + b, 2 * c + d) for a, b, c, d in...]
    pallas_call x3, Pallas kernels: 33 us -> 34.5 us  [call(): pl.pallas_call(kernel, out_shape=outs, in_specs=specs, out_specs=jax.tree...]
  transfers between devices with their start and end apart: 15 -> 17, of which waited for: 3 -> 4; matrix products, arithmetic and copies ran while one was open for 3% -> 0% of each run, Pallas kernels for 25% -> 27%
where the time goes in v2:
time: 80.5 us; the launch traced here: 79.8 us
  Pallas kernels  34.5 us (43%)
  starting transfers between devices  26 us (32%)
  waiting for transfers between devices  15.9 us (20%)
  local copies, waits for them, and re-layouts  1.75 us (2%)
  other arithmetic  1.45 us (2%)
    pallas_call x3, Pallas kernels, call(): pl.pallas_call(kernel, out_shape=outs, in_specs=specs, out_specs=jax.tree...  34.5 us
    ppermute x17, starting transfers between devices, send(): lax.ppermute(x, ('row', 'col'), [(2 * a + b, 2 * c + d) for a, b, c, d in...  26 us
    ppermute x17, waiting for transfers between devices, send(): lax.ppermute(x, ('row', 'col'), [(2 * a + b, 2 * c + d) for a, b, c, d in...  15.9 us
    unnamed x3, local copies, waits for them, and re-layouts  1.73 us
  transfers between devices with their start and end apart: 17, of which 4 were waited for; matrix products, arithmetic and copies ran while one was open for 0% of the time, Pallas kernels for 27%

profile of v2, /device:TPU:25, one launch (start us, length us, event | category | flops | bytes accessed | tf_op | source)
XLA Modules:
  0.0 79.8 jit_solution(14971010662344612239)
XLA Ops:
  0.0 0.7 broadcast_compare_fusion
  0.7 0.1 fusion.3.keep_ref
  0.8 0.1 compare_reduce_fusion
  0.9 1.7 %copy.10 = f32[2,1,4,1,256,256]{5,4,0,2,3,1:T(8,128)S(1)} copy(f32[2,1,4,1,256,256]{5,4,3,2,1,0:T(8,128)} %param.2) | data formatting | bytes 4194304 | tf_op args[0]
  2.6 0.1 fusion.own_ref
  2.8 1.3 %collective-permute-start.5 = (f32[256,256]{1,0:T(8,128)S(1)}, f32[256,256]{1,0:T(8,128)S(1)}, u32[]{:S(2)}, u32[]{:S(2)}) collective-permute-start(f32[256,256]{1,0:T(8,128)S(1)} %slice_bitcast_fusion.1), channel_id=1, source_target_pairs={{4,20},{5,21},{6,22},{7,23},{8,24},{9,25},{10,26},{11,27},{12,28},... | collective-permute-start | bytes 786440 | tf_op jit(solution)/shard_map/ppermute | solution.py:185
  4.1 0.7 collective-permute-start.12
  4.7 0.7 collective-permute-start.1
  5.4 10.1 %collective-permute-done.5 = f32[256,256]{1,0:T(8,128)S(1)} collective-permute-done((f32[256,256]{1,0:T(8,128)S(1)}, f32[256,256]{1,0:T(8,128)S(1)}, u32[]{:S(2)}, u32[]{:S(2)}) %collective-permute-start.5) | collective-permute-done | bytes 262176 | tf_op jit(solution)/shard_map/ppermute | solution.py:185
  15.5 0.0 collective-permute-done.12
  15.5 0.0 collective-permute-done.1
  15.5 0.1 broadcast_select_fusion
  15.6 0.7 collective-permute-start.2
  16.3 1.6 %collective-permute-start = (f32[2,256,256]{2,1,0:T(8,128)S(1)}, f32[2,256,256]{2,1,0:T(8,128)S(1)}, u32[]{:S(2)}, u32[]{:S(2)}) collective-permute-start(f32[2,256,256]{2,1,0:T(8,128)S(1)} %fusion.own_ref), channel_id=1, source_target_pairs={{0,1},{1,0},{2,3},{3,2},{4,5},{5,4},{6,7},{7,6},{8,9},{9,8},{10,11... | collective-permute-start | bytes 1572872 | tf_op jit(solution)/shard_map/ppermute | solution.py:185
  17.9 0.7 collective-permute-start.13
  18.6 0.0 collective-permute-done.2
  18.7 0.7 collective-permute-start.3
  19.3 0.1 pad_add_fusion.place_ref
  19.4 1.9 %collective-permute-start.7 = (f32[256,256]{1,0:T(8,128)S(1)}, f32[256,256]{1,0:T(8,128)S(1)}, u32[]{:S(2)}, u32[]{:S(2)}) collective-permute-start(f32[256,256]{1,0:T(8,128)S(1)} %get-tuple-element.19), channel_id=1, source_target_pairs={{5,6},{6,5},{9,10},{10,9},{13,14},{14,13},{21,22},{22,21},{25,26},... | collective-permute-start | bytes 786440 | tf_op jit(solution)/shard_map/ppermute | solution.py:185
  21.3 1.9 %collective-permute-start.6 = (f32[256,256]{1,0:T(8,128)S(1)}, f32[256,256]{1,0:T(8,128)S(1)}, u32[]{:S(2)}, u32[]{:S(2)}) collective-permute-start(f32[256,256]{1,0:T(8,128)S(1)} %get-tuple-element.19), channel_id=1, source_target_pairs={{4,6},{7,5},{8,10},{11,9},{12,14},{15,13},{20,22},{23,21},{24,26},... | collective-permute-start | bytes 786440 | tf_op jit(solution)/shard_map/ppermute | solution.py:185
  23.3 0.0 collective-permute-done.13
  23.3 0.7 collective-permute-start.14
  24.0 0.0 collective-permute-done.3
  24.1 0.7 collective-permute-start.4
  24.7 3.8 %collective-permute-done.7 = f32[256,256]{1,0:T(8,128)S(1)} collective-permute-done((f32[256,256]{1,0:T(8,128)S(1)}, f32[256,256]{1,0:T(8,128)S(1)}, u32[]{:S(2)}, u32[]{:S(2)}) %collective-permute-start.7) | collective-permute-done | bytes 262176 | tf_op jit(solution)/shard_map/ppermute | solution.py:185
  28.5 1.4 %collective-permute-done.6 = f32[256,256]{1,0:T(8,128)S(1)} collective-permute-done((f32[256,256]{1,0:T(8,128)S(1)}, f32[256,256]{1,0:T(8,128)S(1)}, u32[]{:S(2)}, u32[]{:S(2)}) %collective-permute-start.6) | collective-permute-done | bytes 262176 | tf_op jit(solution)/shard_map/ppermute | solution.py:185
  29.9 0.1 select_bitcast_fusion.1
  30.0 0.0 collective-permute-done.14
  30.0 1.3 %collective-permute-start.15 = (f32[256,256]{1,0:T(8,128)S(1)}, f32[256,256]{1,0:T(8,128)S(1)}, u32[]{:S(2)}, u32[]{:S(2)}) collective-permute-start(f32[256,256]{1,0:T(8,128)S(1)} %broadcast_select_fusion.5), channel_id=1, source_target_pairs={{0,8},{1,9},{2,10},{3,11},{16,24},{17,25},{18,26},{19,27},{4,12},{... | collective-permute-start | bytes 786440 | tf_op jit(solution)/shard_map/ppermute | solution.py:185
  31.3 0.0 collective-permute-done.4
  31.4 1.3 %collective-permute-start.9 = (f32[256,256]{1,0:T(8,128)S(1)}, f32[256,256]{1,0:T(8,128)S(1)}, u32[]{:S(2)}, u32[]{:S(2)}) collective-permute-start(f32[256,256]{1,0:T(8,128)S(1)} %broadcast_select_fusion.8.own_ref), channel_id=1, source_target_pairs={{0,1},{2,3},{4,5},{6,7},{8,9},{10,11},{12,13},{14,15},{16,17},{18,... | collective-permute-start | bytes 786440 | tf_op jit(solution)/shard_map/ppermute | solution.py:185
  32.7 4.0 %collective-permute-start.10 = (f32[2,256,256]{2,1,0:T(8,128)S(1)}, f32[2,256,256]{2,1,0:T(8,128)S(1)}, u32[]{:S(2)}, u32[]{:S(2)}) collective-permute-start(f32[2,256,256]{2,1,0:T(8,128)S(1)} %pad_maximum_fusion.at_ref), channel_id=1, source_target_pairs={{0,8},{1,5},{2,10},{3,7},{4,12},{5,1},{6,14},{7,3},{8,0},{9,13},{1... | collective-permute-start | bytes 1572872 | tf_op jit(solution)/shard_map/ppermute | solution.py:185
  36.7 2.1 %collective-permute-start.8 = (f32[2,256,256]{2,1,0:T(8,128)S(1)}, f32[2,256,256]{2,1,0:T(8,128)S(1)}, u32[]{:S(2)}, u32[]{:S(2)}) collective-permute-start(f32[2,256,256]{2,1,0:T(8,128)S(1)} %pad_maximum_fusion.at_ref), channel_id=1, source_target_pairs={{0,4},{1,9},{2,6},{3,11},{4,0},{5,13},{6,2},{7,15},{8,12},{9,1},{1... | collective-permute-start | bytes 1572872 | tf_op jit(solution)/shard_map/ppermute | solution.py:185
  38.8 0.6 collective-permute-done.15
  39.4 3.0 %collective-permute-start.16 = (f32[256,256]{1,0:T(8,128)S(1)}, f32[256,256]{1,0:T(8,128)S(1)}, u32[]{:S(2)}, u32[]{:S(2)}) collective-permute-start(f32[256,256]{1,0:T(8,128)S(1)} %broadcast_select_fusion.7.own_ref), channel_id=1, source_target_pairs={{0,1},{1,0},{2,3},{3,2},{4,5},{5,4},{6,7},{7,6},{8,9},{9,8},{10,11... | collective-permute-start | bytes 786440 | tf_op jit(solution)/shard_map/ppermute | solution.py:185
  42.4 0.0 collective-permute-done.9.other_ref
  42.4 10.1 %first.1.inv0_ref = f32[256,256]{1,0:T(8,128)S(1)} custom-call(s32[3]{0:T(128)S(1)} %pad_add_fusion.place_ref, f32[256,256]{1,0:T(8,128)S(1)} %broadcast_select_fusion.8.own_ref, f32[256,256]{1,0:T(8,128)S(1)} %collective-permute-done.9.other_ref), custom_call_target="tpu_custom_call" | custom-call | flops 10000000000 | bytes 1048576 | tf_op jit(solution)/shard_map/first/pallas_call | solution.py:158
  52.6 0.0 copy-start
  52.6 0.0 collective-permute-done.8.a_ref
  52.6 2.9 %collective-permute-start.11 = (f32[2,256,256]{2,1,0:T(8,128)S(1)}, f32[2,256,256]{2,1,0:T(8,128)S(1)}, u32[]{:S(2)}, u32[]{:S(2)}) collective-permute-start(f32[2,256,256]{2,1,0:T(8,128)S(1)} %collective-permute-done.8.a_ref), channel_id=1, source_target_pairs={{0,8},{1,5},{2,10},{3,7},{4,12},{5,1},{6,14},{7,3},{8,0},{9,13},{1... | collective-permute-start | bytes 1572872 | tf_op jit(solution)/shard_map/ppermute | solution.py:185
  55.5 0.0 collective-permute-done.16.other_ref
  55.5 11.4 %second.1 = (f32[256,256]{1,0:T(8,128)S(1)}, f32[256,256]{1,0:T(8,128)S(1)}) custom-call(s32[3]{0:T(128)S(1)} %pad_add_fusion.place_ref, f32[256,256]{1,0:T(8,128)S(1)} %broadcast_select_fusion.7.own_ref, f32[256,256]{1,0:T(8,128)S(1)} %collective-permute-done.16.other_ref, f32[256,256]{1,0:T(8,128)S(1)} %first.1.inv0_ref), custom_call_target="tpu_custom_call" | custom-call | flops 10000000000 | bytes 1048576 | tf_op jit(solution)/shard_map/second/pallas_call | solution.py:158
  66.8 0.0 collective-permute-done.other_ref
  66.9 0.0 collective-permute-done.10.b_ref
  66.9 0.0 collective-permute-done.11.c_ref
  66.9 0.0 copy-done
  66.9 13.0 %last.1 = f32[2,4,256,256]{3,2,1,0:T(8,128)} custom-call(s32[3]{0:T(128)S(1)} %pad_add_fusion.place_ref, s32[2,4]{1,0:T(2,128)S(1)} %fusion.3.keep_ref, f32[2,4,256,256]{3,2,1,0:T(8,128)S(1)} %bitcast.33, f32[2,256,256]{2,1,0:T(8,128)S(1)} %fusion.own_ref, f32[2,256,256]{2,1,0:T(8,128)S(1)} %collective-permute-done.other_ref, ...), custom_call_target="tpu_custom_call" | custom-call | flops 10000000000 | bytes 1048576 | tf_op jit(solution)/shard_map/last/pallas_call | solution.py:158
  (10 shorter events, 0.3 us)
Async XLA Ops:
  2.8 12.8 %collective-permute-start.5 = (f32[256,256]{1,0:T(8,128)S(1)}, f32[256,256]{1,0:T(8,128)S(1)}, u32[]{:S(2)}, u32[]{:S(2)}) collective-permute-start(f32[256,256]{1,0:T(8,128)S(1)} %slice_bitcast_fusion.1), channel_id=1, source_target_pairs={{4,20},{5,21},{6,22},{7,23},{8,24},{9,25},{10,26},{11,27},{12,28},... | collective-permute-start | bytes 786440 | tf_op jit(solution)/shard_map/ppermute | solution.py:185
  4.1 11.5 %collective-permute-start.12 = (f32[256,256]{1,0:T(8,128)S(1)}, f32[256,256]{1,0:T(8,128)S(1)}, u32[]{:S(2)}, u32[]{:S(2)}) collective-permute-start(f32[256,256]{1,0:T(8,128)S(1)} %slice_bitcast_fusion.1), channel_id=1, source_target_pairs={{2,0},{3,1}} | collective-permute-start | bytes 786440 | tf_op jit(solution)/shard_map/ppermute | solution.py:185
  4.7 10.8 %collective-permute-start.1 = (f32[256,256]{1,0:T(8,128)S(1)}, f32[256,256]{1,0:T(8,128)S(1)}, u32[]{:S(2)}, u32[]{:S(2)}) collective-permute-start(f32[256,256]{1,0:T(8,128)S(1)} %slice_bitcast_fusion.1), channel_id=1, source_target_pairs={{0,16}} | collective-permute-start | bytes 786440 | tf_op jit(solution)/shard_map/ppermute | solution.py:185
  15.6 3.0 %collective-permute-start.2 = (f32[256,256]{1,0:T(8,128)S(1)}, f32[256,256]{1,0:T(8,128)S(1)}, u32[]{:S(2)}, u32[]{:S(2)}) collective-permute-start(f32[256,256]{1,0:T(8,128)S(1)} %get-tuple-element.18), channel_id=1, source_target_pairs={{0,2},{16,18}} | collective-permute-start | bytes 786440 | tf_op jit(solution)/shard_map/ppermute | solution.py:185
  16.3 50.5 %collective-permute-start = (f32[2,256,256]{2,1,0:T(8,128)S(1)}, f32[2,256,256]{2,1,0:T(8,128)S(1)}, u32[]{:S(2)}, u32[]{:S(2)}) collective-permute-start(f32[2,256,256]{2,1,0:T(8,128)S(1)} %fusion.own_ref), channel_id=1, source_target_pairs={{0,1},{1,0},{2,3},{3,2},{4,5},{5,4},{6,7},{7,6},{8,9},{9,8},{10,11... | collective-permute-start | bytes 1572872 | tf_op jit(solution)/shard_map/ppermute | solution.py:185
  17.9 5.3 %collective-permute-start.13 = (f32[256,256]{1,0:T(8,128)S(1)}, f32[256,256]{1,0:T(8,128)S(1)}, u32[]{:S(2)}, u32[]{:S(2)}) collective-permute-start(f32[256,256]{1,0:T(8,128)S(1)} %get-tuple-element.17), channel_id=1, source_target_pairs={{0,16},{1,17},{2,18},{3,19}} | collective-permute-start | bytes 786440 | tf_op jit(solution)/shard_map/ppermute | solution.py:185
  18.7 5.3 %collective-permute-start.3 = (f32[256,256]{1,0:T(8,128)S(1)}, f32[256,256]{1,0:T(8,128)S(1)}, u32[]{:S(2)}, u32[]{:S(2)}) collective-permute-start(f32[256,256]{1,0:T(8,128)S(1)} %broadcast_select_fusion.4), channel_id=1, source_target_pairs={{0,4},{16,20},{2,6},{18,22}} | collective-permute-start | bytes 786440 | tf_op jit(solution)/shard_map/ppermute | solution.py:185
  19.4 9.1 %collective-permute-start.7 = (f32[256,256]{1,0:T(8,128)S(1)}, f32[256,256]{1,0:T(8,128)S(1)}, u32[]{:S(2)}, u32[]{:S(2)}) collective-permute-start(f32[256,256]{1,0:T(8,128)S(1)} %get-tuple-element.19), channel_id=1, source_target_pairs={{5,6},{6,5},{9,10},{10,9},{13,14},{14,13},{21,22},{22,21},{25,26},... | collective-permute-start | bytes 786440 | tf_op jit(solution)/shard_map/ppermute | solution.py:185
  21.3 8.6 %collective-permute-start.6 = (f32[256,256]{1,0:T(8,128)S(1)}, f32[256,256]{1,0:T(8,128)S(1)}, u32[]{:S(2)}, u32[]{:S(2)}) collective-permute-start(f32[256,256]{1,0:T(8,128)S(1)} %get-tuple-element.19), channel_id=1, source_target_pairs={{4,6},{7,5},{8,10},{11,9},{12,14},{15,13},{20,22},{23,21},{24,26},... | collective-permute-start | bytes 786440 | tf_op jit(solution)/shard_map/ppermute | solution.py:185
  23.3 6.6 %collective-permute-start.14 = (f32[256,256]{1,0:T(8,128)S(1)}, f32[256,256]{1,0:T(8,128)S(1)}, u32[]{:S(2)}, u32[]{:S(2)}) collective-permute-start(f32[256,256]{1,0:T(8,128)S(1)} %broadcast_select_fusion.2), channel_id=1, source_target_pairs={{0,4},{1,5},{2,6},{3,7},{16,20},{17,21},{18,22},{19,23}} | collective-permute-start | bytes 786440 | tf_op jit(solution)/shard_map/ppermute | solution.py:185
  24.1 7.3 %collective-permute-start.4 = (f32[256,256]{1,0:T(8,128)S(1)}, f32[256,256]{1,0:T(8,128)S(1)}, u32[]{:S(2)}, u32[]{:S(2)}) collective-permute-start(f32[256,256]{1,0:T(8,128)S(1)} %broadcast_select_fusion.6), channel_id=1, source_target_pairs={{0,8},{16,24},{2,10},{18,26},{4,12},{20,28},{6,14},{22,30}} | collective-permute-start | bytes 786440 | tf_op jit(solution)/shard_map/ppermute | solution.py:185
  30.0 9.4 %collective-permute-start.15 = (f32[256,256]{1,0:T(8,128)S(1)}, f32[256,256]{1,0:T(8,128)S(1)}, u32[]{:S(2)}, u32[]{:S(2)}) collective-permute-start(f32[256,256]{1,0:T(8,128)S(1)} %broadcast_select_fusion.5), channel_id=1, source_target_pairs={{0,8},{1,9},{2,10},{3,11},{16,24},{17,25},{18,26},{19,27},{4,12},{... | collective-permute-start | bytes 786440 | tf_op jit(solution)/shard_map/ppermute | solution.py:185
  31.4 11.1 %collective-permute-start.9 = (f32[256,256]{1,0:T(8,128)S(1)}, f32[256,256]{1,0:T(8,128)S(1)}, u32[]{:S(2)}, u32[]{:S(2)}) collective-permute-start(f32[256,256]{1,0:T(8,128)S(1)} %broadcast_select_fusion.8.own_ref), channel_id=1, source_target_pairs={{0,1},{2,3},{4,5},{6,7},{8,9},{10,11},{12,13},{14,15},{16,17},{18,... | collective-permute-start | bytes 786440 | tf_op jit(solution)/shard_map/ppermute | solution.py:185
  32.7 34.1 %collective-permute-start.10 = (f32[2,256,256]{2,1,0:T(8,128)S(1)}, f32[2,256,256]{2,1,0:T(8,128)S(1)}, u32[]{:S(2)}, u32[]{:S(2)}) collective-permute-start(f32[2,256,256]{2,1,0:T(8,128)S(1)} %pad_maximum_fusion.at_ref), channel_id=1, source_target_pairs={{0,8},{1,5},{2,10},{3,7},{4,12},{5,1},{6,14},{7,3},{8,0},{9,13},{1... | collective-permute-start | bytes 1572872 | tf_op jit(solution)/shard_map/ppermute | solution.py:185
  36.7 15.9 %collective-permute-start.8 = (f32[2,256,256]{2,1,0:T(8,128)S(1)}, f32[2,256,256]{2,1,0:T(8,128)S(1)}, u32[]{:S(2)}, u32[]{:S(2)}) collective-permute-start(f32[2,256,256]{2,1,0:T(8,128)S(1)} %pad_maximum_fusion.at_ref), channel_id=1, source_target_pairs={{0,4},{1,9},{2,6},{3,11},{4,0},{5,13},{6,2},{7,15},{8,12},{9,1},{1... | collective-permute-start | bytes 1572872 | tf_op jit(solution)/shard_map/ppermute | solution.py:185
  39.4 16.1 %collective-permute-start.16 = (f32[256,256]{1,0:T(8,128)S(1)}, f32[256,256]{1,0:T(8,128)S(1)}, u32[]{:S(2)}, u32[]{:S(2)}) collective-permute-start(f32[256,256]{1,0:T(8,128)S(1)} %broadcast_select_fusion.7.own_ref), channel_id=1, source_target_pairs={{0,1},{1,0},{2,3},{3,2},{4,5},{5,4},{6,7},{7,6},{8,9},{9,8},{10,11... | collective-permute-start | bytes 786440 | tf_op jit(solution)/shard_map/ppermute | solution.py:185
  52.6 14.3 %copy-start = (f32[2,1,4,1,256,256]{5,4,3,2,1,0:T(8,128)S(1)}, f32[2,1,4,1,256,256]{5,4,3,2,1,0:T(8,128)}, u32[]{:S(2)}) copy-start(f32[2,1,4,1,256,256]{5,4,3,2,1,0:T(8,128)} %param.2) | copy-start | bytes 6291460
  52.6 14.3 %collective-permute-start.11 = (f32[2,256,256]{2,1,0:T(8,128)S(1)}, f32[2,256,256]{2,1,0:T(8,128)S(1)}, u32[]{:S(2)}, u32[]{:S(2)}) collective-permute-start(f32[2,256,256]{2,1,0:T(8,128)S(1)} %collective-permute-done.8.a_ref), channel_id=1, source_target_pairs={{0,8},{1,5},{2,10},{3,7},{4,12},{5,1},{6,14},{7,3},{8,0},{9,13},{1... | collective-permute-start | bytes 1572872 | tf_op jit(solution)/shard_map/ppermute | solution.py:185

commit v3 on v2

v3 whole, which is shorter than its diff:
```python
import jax
import jax.numpy as jnp
from jax import lax
from jax.experimental import pallas as pl
from jax.experimental.pallas import tpu as pltpu
from jax.sharding import PartitionSpec as P

HALF_BAND = 256
F32 = jnp.float32
BF16 = jnp.bfloat16
VMEM = pl.BlockSpec(memory_space=pltpu.VMEM)
ANY = pl.BlockSpec(memory_space=pl.ANY)
SMEM = pl.BlockSpec(memory_space=pltpu.SMEM)
STEPS = 17 * 16 * 8 + 8


def product(a, b):
    return lax.dot_general(a, b, (((1,), (1,)), ((), ())), preferred_element_type=F32)


def thirds(x):
    high = x.astype(BF16)
    rest = x - high.astype(F32)
    middle = rest.astype(BF16)
    return high, middle, (rest - middle.astype(F32)).astype(BF16)


def left6(x):
    h, m, l = thirds(x)
    return jnp.concatenate([h, h, m, h, l, m], 1)


def right6(x):
    h, m, l = thirds(x)
    return jnp.concatenate([h, m, h, l, h, m], 1)


def left3(x):
    h, m, _ = thirds(x)
    return jnp.concatenate([h, h, m], 1)


def right3(x):
    h, m, _ = thirds(x)
    return jnp.concatenate([h, m, h], 1)


def dot(a, b, da, db):
    return lax.dot_general(
        a,
        b,
        (((da,), (db,)), ((), ())),
        precision=lax.Precision.HIGHEST,
        preferred_element_type=F32,
    )


def lanes(x, j):
    return jnp.broadcast_to(x[:, j : j + 1], x.shape)


def inverse128(a, steps_ref):
    n = a.shape[0] // 8
    sub = lax.broadcasted_iota(jnp.int32, (8, 128), 0)
    lane = lax.broadcasted_iota(jnp.int32, (8, 128), 1)
    count = [0]

    def keep(x):
        at = 8 * count[0]
        count[0] += 1
        steps_ref[at : at + 8, :] = x
        return at

    def row(at, r):
        return steps_ref[pl.ds(at + r, 8, stride=0), :]

    part = [a[8 * i : 8 * i + 8, :] for i in range(n)]
    column = [lanes(part[0], c) for c in range(8)]
    inverse = []
    for k in range(n):
        here = (lane >= 8 * k) & (lane < 8 * k + 8)
        kept = [keep(c) for c in column]
        pivot = {(r, s): row(kept[s], r) for s in range(8) for r in range(s, 8)}
        low, scale, solved = {}, [], []
        if k + 1 < n:
            below = [lanes(part[k + 1], 8 * k + s) for s in range(8)]
            column = [lanes(part[k + 1], 8 * k + 8 + c) for c in range(8)]
        for s in range(8):
            reciprocal = 1.0 / pivot[s, s]
            scale.append(lax.rsqrt(pivot[s, s]))
            for r in range(s + 1, 8):
                low[r, s] = pivot[r, s] * scale[s]
            for t in range(s + 1, 8):
                for r in range(t, 8):
                    pivot[r, t] = pivot[r, t] - (pivot[r, s] * pivot[t, s]) * reciprocal
            if k + 1 < n:
                x = below[s]
                for t in range(s):
                    x = x - low[s, t] * solved[t]
                x = x * scale[s]
                solved.append(x)
                at = keep(x)
                for c in range(8):
                    column[c] = column[c] - x * row(at, c)
        at = keep(jnp.where(here, jnp.where(lane == sub + 8 * k, 1.0, 0.0).astype(F32), part[k]))
        u = []
        for s in range(8):
            x = row(at, s)
            for t in range(s):
                x = x - low[s, t] * u[t]
            u.append(x * scale[s])
        x = u[7]
        for s in range(6, -1, -1):
            x = jnp.where(sub == s, u[s], x)
        inverse.append(jnp.where(lane <= sub + 8 * k, x, 0.0))
        if k + 1 < n:
            x = jnp.where(here, 0.0, part[k + 1])
            for s in range(8):
                x = x - solved[s] * u[s]
            part[k + 1] = x
        if k + 2 < n:
            for s in range(7, -1, -1):
                for t in range(s + 1, 8):
                    u[s] = u[s] - low[t, s] * u[t]
                u[s] = u[s] * scale[s]
            for i in range(k + 2, n):
                x = jnp.where(here, 0.0, part[i])
                for s in range(8):
                    x = x - lanes(part[i], 8 * k + s) * u[s]
                part[i] = x
    return jnp.concatenate(inverse, 0)


def inverse_factor(a_ref, out_ref, steps_ref):
    h = a_ref.shape[0] // 2
    inv0 = inverse128(a_ref[:h, :h], steps_ref)
    upper = dot(inv0, a_ref[:h, h:], 1, 0)
    inv1 = inverse128(a_ref[h:, h:] - dot(upper, upper, 0, 0), steps_ref)
    out_ref[:h, :h] = inv0
    out_ref[:h, h:] = jnp.zeros((h, h), F32)
    out_ref[h:, :h] = -dot(inv1, dot(upper, inv0, 0, 0), 1, 0)
    out_ref[h:, h:] = inv1


def first_kernel(place_ref, tile_ref, out_ref, steps_ref):
    root = (place_ref[0] == 0) & (place_ref[1] == 0)

    @pl.when(root)
    def _():
        inverse_factor(tile_ref, out_ref, steps_ref)

    @pl.when(jnp.logical_not(root))
    def _():
        out_ref[...] = tile_ref[...]


def second_kernel(place_ref, own_ref, other_ref, inv0_ref, low_ref, inv1_ref, tile_ref, steps_ref):
    first = place_ref[1] == 0
    inv0 = jnp.where(first, own_ref[0], other_ref[0])
    inv0_ref[...] = inv0
    low = product(left6(jnp.where(first, own_ref[1], other_ref[1])), right6(inv0))
    low_ref[...] = low
    corner = jnp.where(first, other_ref[0], own_ref[0])
    tile_ref[...] = corner - product(left6(low), right6(low))
    inverse_factor(tile_ref, inv1_ref, steps_ref)


def last_kernel(
    place_ref, keep_ref, inv0_ref, low_ref, inv1_ref, own_ref, other_ref, at_ref, a_ref, b_ref, c_ref,
    tiles_ref, out_ref, own, other, hops, tiles, result, sems, hop_sems, out_sems,
):
    p, q = place_ref[0], place_ref[1]
    edge, count, pairs = tiles_ref.shape[-1], tiles_ref.shape[0], tiles_ref.shape[1]
    copy = pltpu.make_async_copy
    loads = [
        copy(own_ref, own, sems.at[0]),
        copy(other_ref, other, sems.at[1]),
        copy(tiles_ref, tiles, sems.at[2]),
    ]
    hop_loads = [
        copy(ref, hops.at[i], hop_sems.at[i]) for i, ref in enumerate((at_ref, a_ref, b_ref, c_ref))
    ]
    for load in loads[:2] + hop_loads + loads[2:]:
        load.start()
    row = lax.broadcasted_iota(jnp.int32, (edge, edge), 0)
    lower = row >= lax.broadcasted_iota(jnp.int32, (edge, edge), 1)
    inv0, low, inv1 = right6(inv0_ref[...]), right6(low_ref[...]), right6(inv1_ref[...])

    def solve(left, right):
        first = product(left6(left), inv0)
        return first, product(left6(right - product(left6(first), low)), inv1)

    for load in loads[:2] + hop_loads:
        load.wait()
    rows, panels = [], []
    for t in range(count):
        i = t * place_ref[2] + p
        first, second = solve(
            jnp.where(q == 0, own[t], other[t]), jnp.where(q == 0, other[t], own[t])
        )
        first = jnp.where((i > 0) | lower, first, 0.0)
        second = jnp.where((i > 1) | ((i == 1) & lower), second, 0.0)
        result[t, 0] = jnp.where(q == 0, first, second)
        rows.append(left3(jnp.concatenate([first, second], 1)))
    for i in range(4):
        first, second = solve(
            jnp.where(q == 0, hops[i, 0], hops[i, 1]), jnp.where(q == 0, hops[i, 1], hops[i, 0])
        )
        panels.append(right3(jnp.concatenate([first, second], 1)))
    loads[2].wait()
    for i in range(4):
        flip = jnp.where(q == 0, i, (i % 2) * 2 + i // 2)
        s = jnp.bitwise_xor(lax.rem(p, 8) // 2, flip)
        room = jnp.where(s > 0, s, pairs)
        for t in range(count):
            wanted = 2 * s + q <= t * place_ref[2] + p
            tile = jnp.where(keep_ref[t, s] == 1, tiles[t, s], 0.0)
            result[t, room] = tile - jnp.where(wanted, product(rows[t], panels[i]), 0.0)

    for t in range(count):
        copy(result.at[t, pl.ds(0, pairs)], out_ref.at[t], out_sems.at[t]).start()
    for t in range(count):
        copy(result.at[t, pl.ds(0, pairs)], out_ref.at[t], out_sems.at[t]).wait()


def call(kernel, name, outs, specs, scratch, flops, *args, out_specs=VMEM):
    return pl.pallas_call(
        kernel,
        out_shape=outs,
        in_specs=specs,
        out_specs=out_specs,
        scratch_shapes=scratch,
        name=name,
        cost_estimate=pl.CostEstimate(flops=flops, bytes_accessed=1 << 20, transcendentals=0),
        compiler_params=pltpu.CompilerParams(vmem_limit_bytes=48 << 20),
    )(*args)


def after(x, *earlier):
    return lax.optimization_barrier((x,) + earlier)[0]


def local(matrix, keep_mask):
    tiles = matrix[:, 0, :, 0]
    row_count, pair_count, edge = tiles.shape[0], tiles.shape[1], tiles.shape[-1]
    n = lax.axis_size("row")
    p, q = lax.axis_index("row"), lax.axis_index("col")
    tile_row = jnp.arange(row_count, dtype=jnp.int32)[:, None] * n + p
    tile_col = 2 * jnp.arange(pair_count, dtype=jnp.int32)[None, :] + q
    keep = (
        ((keep_mask[:, 0, :, 0] == 1) | (tile_row == tile_col))
        & (tile_row >= tile_col)
        & (tile_row - tile_col <= HALF_BAND)
    ).astype(jnp.int32)
    place = jnp.stack([p, q, jnp.int32(n)]).astype(jnp.int32)

    def send(x, pairs):
        return lax.ppermute(x, ("row", "col"), [(2 * a + b, 2 * c + d) for a, b, c, d in pairs])

    mine = jnp.where(keep[0, 0] == 1, matrix[0, 0, 0, 0], 0.0)
    high = []
    while 8 << len(high) < n:
        high.append(8 << len(high))
    sources = [i for i in range(n) if i % 8 > 1]
    flips = (2, 4)

    def chosen(ps):
        return sum([(p == i).astype(jnp.int32) for i in ps]) > 0

    source = [(0, 0), (1, 0), (1, 1)]
    tile = jax.ShapeDtypeStruct((edge, edge), F32)
    room = pltpu.VMEM((STEPS, edge // 2), F32)
    held = call(first_kernel, "first", tile, [SMEM, VMEM], [room], 10**9, place, mine)
    for bit in high[1:]:
        r = send(held, [(i, c, i + bit, c) for i, c in source])
        held = jnp.where(chosen([i + bit for i, _ in source]), r, held)
        source = source + [(i + bit, c) for i, c in source]
    steps = (2, high[0], high[0] + 2)
    received = [send(held, [(i, c, i + bit, c) for i, c in source]) for bit in steps]
    trail = mine
    for size in high:
        r = send(trail, [(i, c, i + size, c) for i in range(2, size) if i % 8 > 1 for c in range(2)])
        trail = jnp.where((p >= size) & (p < 2 * size), r, trail)
    for bit, r in zip(steps, received):
        held = jnp.where(chosen([i + bit for i, _ in source]), r, held)
    source = source + [(i + bit, c) for bit in steps for i, c in source]
    across = send(held, [(i, c, i ^ 1, c) for i, c in source])
    up = send(held, [(i, c, i + 4, c) for i, c in source])
    both = send(held, [(i, c, (i ^ 1) + 4, c) for i, c in source])
    below, even = jnp.bitwise_and(p, 4) == 0, jnp.bitwise_and(p, 1) == 0
    straight, crossed = jnp.where(below, held, up), jnp.where(below, across, both)
    row0 = jnp.where(even, straight, crossed)
    row1 = jnp.where(even, crossed, straight)
    lead = jnp.stack([jnp.where(q == 0, row0, row1), row1])

    r1 = send(
        trail,
        [(i, i % 2, i ^ 1, i % 2) for i in sources] + [(i, 1 - i % 2, i, i % 2) for i in sources],
    )
    r2 = send(trail, [(i, 1 - i % 2, i ^ 1, i % 2) for i in sources])
    lead_other = send(lead, [(i, c, i, 1 - c) for i in range(n) for c in range(2)])
    home = jnp.bitwise_and(p, 1) == q
    at = jnp.stack([jnp.where(home, trail, r1), jnp.where(home, r1, r2)])
    ra = send(at, [(i, c, i ^ flips[c], c) for i in range(n) for c in range(2)])
    rb = send(at, [(i, c, i ^ flips[1 - c], c) for i in range(n) for c in range(2)])

    lead, at = lax.optimization_barrier((lead, at))
    inv0, low, inv1 = call(
        second_kernel, "second", [tile, tile, tile], [SMEM, VMEM, VMEM],
        [pltpu.VMEM((edge, edge), F32), room], 10**10, place, lead, lead_other, out_specs=[VMEM] * 3,
    )
    rc = send(ra, [(i, c, i ^ flips[1 - c], c) for i in range(n) for c in range(2)])
    own = jnp.stack([mine, jnp.where(keep[1, 0] == 1, matrix[1, 0, 0, 0], 0.0)])
    other = send(after(own, inv1), [(i, c, i, 1 - c) for i in range(n) for c in range(2)])
    out = call(
        last_kernel, "last", jax.ShapeDtypeStruct(tiles.shape, F32),
        [SMEM, SMEM, VMEM, VMEM, VMEM] + [ANY] * 7,
        [
            pltpu.VMEM(own.shape, F32),
            pltpu.VMEM(own.shape, F32),
            pltpu.VMEM((4,) + at.shape, F32),
            pltpu.VMEM(tiles.shape, F32),
            pltpu.VMEM((row_count, pair_count + 1, edge, edge), F32),
            pltpu.SemaphoreType.DMA((3,)),
            pltpu.SemaphoreType.DMA((4,)),
            pltpu.SemaphoreType.DMA((row_count,)),
        ],
        10**10, place, keep, inv0, low, inv1, own, other, at, ra, rb, rc, tiles, out_specs=ANY,
    )
    return out[:, None, :, None]


def solution(mesh):
    return jax.shard_map(
        local,
        mesh=mesh,
        in_specs=(P(None, "row", None, "col", None, None), P(None, "row", None, "col")),
        out_specs=P(None, "row", None, "col", None, None),
        check_vma=False,
    )
```

time: 80.5 us -> 71.8 us (0.89)
  Pallas kernels: 34.5 us -> 18.8 us
  waiting for transfers between devices: 15.9 us -> 29.2 us
  starting transfers between devices: 26 us -> 18.3 us
  between operations: 0.29 us -> 1.61 us
  local copies, waits for them, and re-layouts: 1.75 us -> 0.56 us
  other arithmetic: 1.45 us -> 2.33 us
    pallas_call x3, Pallas kernels: 34.5 us -> 18.8 us  [call(): pl.pallas_call(kernel, out_shape=outs, in_specs=specs, out_specs=out_spec...]
    ppermute x17 -> x14, waiting for transfers between devices: 15.9 us -> 29.2 us  [send(): lax.ppermute(x, ('row', 'col'), [(2 * a + b, 2 * c + d) for a, b, c, d in...]
    ppermute x17 -> x14, starting transfers between devices: 26 us -> 18.3 us  [send(): lax.ppermute(x, ('row', 'col'), [(2 * a + b, 2 * c + d) for a, b, c, d in...]
    unnamed x3 -> x2, local copies, waits for them, and re-layouts: 1.73 us -> 0.01 us
    select_n x8 -> x3, other arithmetic: 0.4 us -> 1.22 us  [the longest x1 1.08 us: local(): mine = jnp.where(keep[0, 0] == 1, matrix[0, 0, 0, 0], 0.0)]
  transfers between devices with their start and end apart: 17 -> 14, of which waited for: 4 -> 5; matrix products, arithmetic and copies ran while one was open for 0% -> 1% of each run, Pallas kernels for 27% -> 11%
where the time goes in v3:
time: 71.8 us; the launch traced here: 70.8 us
  waiting for transfers between devices  29.2 us (41%)
  Pallas kernels  18.8 us (26%)
  starting transfers between devices  18.3 us (25%)
  other arithmetic  2.33 us (3%)
  between operations  1.61 us (2%)
    ppermute x14, waiting for transfers between devices, send(): lax.ppermute(x, ('row', 'col'), [(2 * a + b, 2 * c + d) for a, b, c, d in...  29.2 us
    pallas_call x3, Pallas kernels, call(): pl.pallas_call(kernel, out_shape=outs, in_specs=specs, out_specs=out_spec...  18.8 us
    ppermute x14, starting transfers between devices, send(): lax.ppermute(x, ('row', 'col'), [(2 * a + b, 2 * c + d) for a, b, c, d in...  18.3 us
  transfers between devices with their start and end apart: 14, of which 5 were waited for; matrix products, arithmetic and copies ran while one was open for 1% of the time, Pallas kernels for 11%

profile of v3, /device:TPU:25, one launch (start us, length us, event | category | flops | bytes accessed | tf_op | source)
XLA Modules:
  0.0 70.8 jit_solution(11848970773101243665)
XLA Ops:
  0.0 0.7 broadcast_compare_fusion
  0.7 0.1 fusion.5.keep_ref
  0.8 0.5 fusion.6
  2.5 0.1 pad_add_fusion.place_ref
  2.6 1.1 %fusion = (f32[1,256,256]{2,1,0:T(8,128)S(1)}, f32[256,256]{1,0:T(8,128)S(1)}, f32[1,256,256]{2,1,0:T(8,128)S(1)}) fusion(f32[2,1,4,1,256,256]{5,4,3,2,1,0:T(8,128)} %param.2, pred[]{:T(512)} %bitcast.2, pred[]{:T(512)} %bitcast.9), kind=kLoop, calls=%fused_computation.9 | loop fusion | flops 131072 | bytes 1310722 | tf_op jit(solution)/shard_map/jit(_where)/select_n | solution.py:260
  3.7 0.6 first.1
  4.3 0.7 collective-permute-start.2
  4.9 0.7 collective-permute-start.1
  5.6 0.7 collective-permute-start
  6.3 1.3 %collective-permute-start.6 = (f32[256,256]{1,0:T(8,128)S(1)}, f32[256,256]{1,0:T(8,128)S(1)}, u32[]{:S(2)}, u32[]{:S(2)}) collective-permute-start(f32[256,256]{1,0:T(8,128)S(1)} %get-tuple-element.18.tile_ref), channel_id=1, source_target_pairs={{4,20},{5,21},{6,22},{7,23},{8,24},{9,25},{10,26},{11,27},{12,28},... | collective-permute-start | bytes 786440 | tf_op jit(solution)/shard_map/ppermute | solution.py:258
  7.6 0.0 collective-permute-done.2
  7.7 0.0 collective-permute-done.1
  7.7 0.0 collective-permute-done
  7.7 0.1 select_select_fusion
  7.8 1.3 %collective-permute-start.5 = (f32[256,256]{1,0:T(8,128)S(1)}, f32[256,256]{1,0:T(8,128)S(1)}, u32[]{:S(2)}, u32[]{:S(2)}) collective-permute-start(f32[256,256]{1,0:T(8,128)S(1)} %select_select_fusion), channel_id=1, source_target_pairs={{0,10},{2,8},{3,9},{4,14},{6,12},{7,13},{16,26},{18,24},{19,25},{2... | collective-permute-start | bytes 786440 | tf_op jit(solution)/shard_map/ppermute | solution.py:258
  9.1 0.7 collective-permute-start.4
  9.8 0.7 collective-permute-start.3
  10.5 11.5 %collective-permute-done.6 = f32[256,256]{1,0:T(8,128)S(1)} collective-permute-done((f32[256,256]{1,0:T(8,128)S(1)}, f32[256,256]{1,0:T(8,128)S(1)}, u32[]{:S(2)}, u32[]{:S(2)}) %collective-permute-start.6) | collective-permute-done | bytes 262176 | tf_op jit(solution)/shard_map/ppermute | solution.py:258
  22.0 8.7 %collective-permute-start.8 = (f32[256,256]{1,0:T(8,128)S(1)}, f32[256,256]{1,0:T(8,128)S(1)}, u32[]{:S(2)}, u32[]{:S(2)}) collective-permute-start(f32[256,256]{1,0:T(8,128)S(1)} %broadcast_select_fusion), channel_id=1, source_target_pairs={{5,6},{6,5},{9,10},{10,9},{13,14},{14,13},{21,22},{22,21},{25,26},... | collective-permute-start | bytes 786440 | tf_op jit(solution)/shard_map/ppermute | solution.py:258
  30.7 2.1 %collective-permute-start.7 = (f32[256,256]{1,0:T(8,128)S(1)}, f32[256,256]{1,0:T(8,128)S(1)}, u32[]{:S(2)}, u32[]{:S(2)}) collective-permute-start(f32[256,256]{1,0:T(8,128)S(1)} %broadcast_select_fusion), channel_id=1, source_target_pairs={{4,6},{7,5},{8,10},{11,9},{12,14},{15,13},{20,22},{23,21},{24,26},... | collective-permute-start | bytes 786440 | tf_op jit(solution)/shard_map/ppermute | solution.py:258
  32.8 0.0 collective-permute-done.5
  32.9 0.0 collective-permute-done.4
  32.9 0.0 collective-permute-done.3
  32.9 0.1 select_bitcast_fusion.3
  33.0 0.5 collective-permute-start.9
  33.5 1.5 %collective-permute-done.8 = f32[256,256]{1,0:T(8,128)S(1)} collective-permute-done((f32[256,256]{1,0:T(8,128)S(1)}, f32[256,256]{1,0:T(8,128)S(1)}, u32[]{:S(2)}, u32[]{:S(2)}) %collective-permute-start.8) | collective-permute-done | bytes 262176 | tf_op jit(solution)/shard_map/ppermute | solution.py:258
  35.0 2.8 %collective-permute-done.7 = f32[256,256]{1,0:T(8,128)S(1)} collective-permute-done((f32[256,256]{1,0:T(8,128)S(1)}, f32[256,256]{1,0:T(8,128)S(1)}, u32[]{:S(2)}, u32[]{:S(2)}) %collective-permute-start.7) | collective-permute-done | bytes 262176 | tf_op jit(solution)/shard_map/ppermute | solution.py:258
  37.9 0.1 select_bitcast_fusion.2
  38.0 0.0 copy-start
  38.0 0.1 collective-permute-start.12
  38.0 0.5 collective-permute-start.11
  38.6 0.0 collective-permute-done.9.other_ref
  38.6 7.8 %second.1 = (f32[256,256]{1,0:T(8,128)S(1)}, f32[256,256]{1,0:T(8,128)S(1)}, f32[256,256]{1,0:T(8,128)S(1)}) custom-call(s32[3]{0:T(128)S(1)} %pad_add_fusion.place_ref, f32[2,256,256]{2,1,0:T(8,128)S(1)} %pad_maximum_fusion.own_ref, f32[2,256,256]{2,1,0:T(8,128)S(1)} %collective-permute-done.9.other_ref), custom_call_target="tpu_custom_call" | custom-call | flops 10000000000 | bytes 1048576 | tf_op jit(solution)/shard_map/second/pallas_call | solution.py:227
  46.3 5.5 %collective-permute-done.11.a_ref = f32[2,256,256]{2,1,0:T(8,128)S(1)} collective-permute-done((f32[2,256,256]{2,1,0:T(8,128)S(1)}, f32[2,256,256]{2,1,0:T(8,128)S(1)}, u32[]{:S(2)}, u32[]{:S(2)}) %collective-permute-start.11) | collective-permute-done | bytes 524320 | tf_op jit(solution)/shard_map/ppermute | solution.py:258
  51.8 0.0 collective-permute-start.13
  51.8 0.4 collective-permute-start.10
  52.2 0.0 collective-permute-done.12.b_ref
  52.2 7.9 %collective-permute-done.13.c_ref = f32[2,256,256]{2,1,0:T(8,128)S(1)} collective-permute-done((f32[2,256,256]{2,1,0:T(8,128)S(1)}, f32[2,256,256]{2,1,0:T(8,128)S(1)}, u32[]{:S(2)}, u32[]{:S(2)}) %collective-permute-start.13) | collective-permute-done | bytes 524320 | tf_op jit(solution)/shard_map/ppermute | solution.py:258
  60.1 0.0 collective-permute-done.10.other_ref
  60.1 0.0 copy-done
  60.1 10.5 %last.1 = f32[2,4,256,256]{3,2,1,0:T(8,128)} custom-call(s32[3]{0:T(128)S(1)} %pad_add_fusion.place_ref, s32[2,4]{1,0:T(2,128)S(1)} %fusion.5.keep_ref, f32[256,256]{1,0:T(8,128)S(1)} %get-tuple-element.12.inv0_ref, f32[256,256]{1,0:T(8,128)S(1)} %get-tuple-element.13.low_ref, f32[256,256]{1,0:T(8,128)S(1)} %get-tuple-element.14.inv1_ref, ...), custom_call_target="tpu_custom_call" | custom-call | flops 10000000000 | bytes 1048576 | tf_op jit(solution)/shard_map/last/pallas_call | solution.py:227
  (6 shorter events, 0.1 us)
Async XLA Ops:
  4.3 3.4 %collective-permute-start.2 = (f32[256,256]{1,0:T(8,128)S(1)}, f32[256,256]{1,0:T(8,128)S(1)}, u32[]{:S(2)}, u32[]{:S(2)}) collective-permute-start(f32[256,256]{1,0:T(8,128)S(1)} %first.1), channel_id=1, source_target_pairs={{0,4},{2,6},{3,7}} | collective-permute-start | bytes 786440 | tf_op jit(solution)/shard_map/ppermute | solution.py:258
  4.9 2.7 %collective-permute-start.1 = (f32[256,256]{1,0:T(8,128)S(1)}, f32[256,256]{1,0:T(8,128)S(1)}, u32[]{:S(2)}, u32[]{:S(2)}) collective-permute-start(f32[256,256]{1,0:T(8,128)S(1)} %first.1), channel_id=1, source_target_pairs={{0,16},{2,18},{3,19}} | collective-permute-start | bytes 786440 | tf_op jit(solution)/shard_map/ppermute | solution.py:258
  5.6 2.0 %collective-permute-start = (f32[256,256]{1,0:T(8,128)S(1)}, f32[256,256]{1,0:T(8,128)S(1)}, u32[]{:S(2)}, u32[]{:S(2)}) collective-permute-start(f32[256,256]{1,0:T(8,128)S(1)} %first.1), channel_id=1, source_target_pairs={{0,20},{2,22},{3,23}} | collective-permute-start | bytes 786440 | tf_op jit(solution)/shard_map/ppermute | solution.py:258
  6.3 15.6 %collective-permute-start.6 = (f32[256,256]{1,0:T(8,128)S(1)}, f32[256,256]{1,0:T(8,128)S(1)}, u32[]{:S(2)}, u32[]{:S(2)}) collective-permute-start(f32[256,256]{1,0:T(8,128)S(1)} %get-tuple-element.18.tile_ref), channel_id=1, source_target_pairs={{4,20},{5,21},{6,22},{7,23},{8,24},{9,25},{10,26},{11,27},{12,28},... | collective-permute-start | bytes 786440 | tf_op jit(solution)/shard_map/ppermute | solution.py:258
  7.8 25.1 %collective-permute-start.5 = (f32[256,256]{1,0:T(8,128)S(1)}, f32[256,256]{1,0:T(8,128)S(1)}, u32[]{:S(2)}, u32[]{:S(2)}) collective-permute-start(f32[256,256]{1,0:T(8,128)S(1)} %select_select_fusion), channel_id=1, source_target_pairs={{0,10},{2,8},{3,9},{4,14},{6,12},{7,13},{16,26},{18,24},{19,25},{2... | collective-permute-start | bytes 786440 | tf_op jit(solution)/shard_map/ppermute | solution.py:258
  9.1 23.8 %collective-permute-start.4 = (f32[256,256]{1,0:T(8,128)S(1)}, f32[256,256]{1,0:T(8,128)S(1)}, u32[]{:S(2)}, u32[]{:S(2)}) collective-permute-start(f32[256,256]{1,0:T(8,128)S(1)} %select_select_fusion), channel_id=1, source_target_pairs={{0,2},{2,0},{3,1},{4,6},{6,4},{7,5},{16,18},{18,16},{19,17},{20,22... | collective-permute-start | bytes 786440 | tf_op jit(solution)/shard_map/ppermute | solution.py:258
  9.8 23.1 %collective-permute-start.3 = (f32[256,256]{1,0:T(8,128)S(1)}, f32[256,256]{1,0:T(8,128)S(1)}, u32[]{:S(2)}, u32[]{:S(2)}) collective-permute-start(f32[256,256]{1,0:T(8,128)S(1)} %select_select_fusion), channel_id=1, source_target_pairs={{0,8},{2,10},{3,11},{4,12},{6,14},{7,15},{16,24},{18,26},{19,27},{... | collective-permute-start | bytes 786440 | tf_op jit(solution)/shard_map/ppermute | solution.py:258
  22.0 13.1 %collective-permute-start.8 = (f32[256,256]{1,0:T(8,128)S(1)}, f32[256,256]{1,0:T(8,128)S(1)}, u32[]{:S(2)}, u32[]{:S(2)}) collective-permute-start(f32[256,256]{1,0:T(8,128)S(1)} %broadcast_select_fusion), channel_id=1, source_target_pairs={{5,6},{6,5},{9,10},{10,9},{13,14},{14,13},{21,22},{22,21},{25,26},... | collective-permute-start | bytes 786440 | tf_op jit(solution)/shard_map/ppermute | solution.py:258
  30.7 7.1 %collective-permute-start.7 = (f32[256,256]{1,0:T(8,128)S(1)}, f32[256,256]{1,0:T(8,128)S(1)}, u32[]{:S(2)}, u32[]{:S(2)}) collective-permute-start(f32[256,256]{1,0:T(8,128)S(1)} %broadcast_select_fusion), channel_id=1, source_target_pairs={{4,6},{7,5},{8,10},{11,9},{12,14},{15,13},{20,22},{23,21},{24,26},... | collective-permute-start | bytes 786440 | tf_op jit(solution)/shard_map/ppermute | solution.py:258
  33.0 5.5 %collective-permute-start.9 = (f32[2,256,256]{2,1,0:T(8,128)S(1)}, f32[2,256,256]{2,1,0:T(8,128)S(1)}, u32[]{:S(2)}, u32[]{:S(2)}) collective-permute-start(f32[2,256,256]{2,1,0:T(8,128)S(1)} %pad_maximum_fusion.own_ref), channel_id=1, source_target_pairs={{0,1},{1,0},{2,3},{3,2},{4,5},{5,4},{6,7},{7,6},{8,9},{9,8},{10,11... | collective-permute-start | bytes 1572872 | tf_op jit(solution)/shard_map/ppermute | solution.py:258
  38.0 22.2 %copy-start = (f32[2,1,4,1,256,256]{5,4,3,2,1,0:T(8,128)S(1)}, f32[2,1,4,1,256,256]{5,4,3,2,1,0:T(8,128)}, u32[]{:S(2)}) copy-start(f32[2,1,4,1,256,256]{5,4,3,2,1,0:T(8,128)} %param.2) | copy-start | bytes 6291460
  38.0 14.2 %collective-permute-start.12 = (f32[2,256,256]{2,1,0:T(8,128)S(1)}, f32[2,256,256]{2,1,0:T(8,128)S(1)}, u32[]{:S(2)}, u32[]{:S(2)}) collective-permute-start(f32[2,256,256]{2,1,0:T(8,128)S(1)} %pad_maximum_fusion.1.at_ref), channel_id=1, source_target_pairs={{0,8},{1,5},{2,10},{3,7},{4,12},{5,1},{6,14},{7,3},{8,0},{9,13},{1... | collective-permute-start | bytes 1572872 | tf_op jit(solution)/shard_map/ppermute | solution.py:258
  38.0 13.7 %collective-permute-start.11 = (f32[2,256,256]{2,1,0:T(8,128)S(1)}, f32[2,256,256]{2,1,0:T(8,128)S(1)}, u32[]{:S(2)}, u32[]{:S(2)}) collective-permute-start(f32[2,256,256]{2,1,0:T(8,128)S(1)} %pad_maximum_fusion.1.at_ref), channel_id=1, source_target_pairs={{0,4},{1,9},{2,6},{3,11},{4,0},{5,13},{6,2},{7,15},{8,12},{9,1},{1... | collective-permute-start | bytes 1572872 | tf_op jit(solution)/shard_map/ppermute | solution.py:258
  51.8 8.3 %collective-permute-start.13 = (f32[2,256,256]{2,1,0:T(8,128)S(1)}, f32[2,256,256]{2,1,0:T(8,128)S(1)}, u32[]{:S(2)}, u32[]{:S(2)}) collective-permute-start(f32[2,256,256]{2,1,0:T(8,128)S(1)} %collective-permute-done.11.a_ref), channel_id=1, source_target_pairs={{0,8},{1,5},{2,10},{3,7},{4,12},{5,1},{6,14},{7,3},{8,0},{9,13},{1... | collective-permute-start | bytes 1572872 | tf_op jit(solution)/shard_map/ppermute | solution.py:258
  51.8 8.3 %collective-permute-start.10 = (f32[2,256,256]{2,1,0:T(8,128)S(1)}, f32[2,256,256]{2,1,0:T(8,128)S(1)}, u32[]{:S(2)}, u32[]{:S(2)}) collective-permute-start(f32[2,256,256]{2,1,0:T(8,128)S(1)} %pad_maximum_fusion.2.own_ref), channel_id=1, source_target_pairs={{0,1},{1,0},{2,3},{3,2},{4,5},{5,4},{6,7},{7,6},{8,9},{9,8},{10,11... | collective-permute-start | bytes 1572872 | tf_op jit(solution)/shard_map/ppermute | solution.py:258

commit v4 on v3

--- a/solution.py
+++ b/solution.py
@@ -154,6 +154,11 @@
         out_ref[...] = tile_ref[...]
 
 
+def solve(left, right, inv0, low, inv1):
+    first = product(left6(left), inv0)
+    return first, product(left6(right - product(left6(first), low)), inv1)
+
+
 def second_kernel(place_ref, own_ref, other_ref, inv0_ref, low_ref, inv1_ref, tile_ref, steps_ref):
     first = place_ref[1] == 0
     inv0 = jnp.where(first, own_ref[0], other_ref[0])
@@ -165,70 +170,108 @@
     inverse_factor(tile_ref, inv1_ref, steps_ref)
 
 
-def last_kernel(
-    place_ref, keep_ref, inv0_ref, low_ref, inv1_ref, own_ref, other_ref, at_ref, a_ref, b_ref, c_ref,
-    tiles_ref, out_ref, own, other, hops, tiles, result, sems, hop_sems, out_sems,
+def slot_of(place_ref, hop):
+    flip = jnp.where(place_ref[1] == 0, hop, (hop % 2) * 2 + hop // 2)
+    return jnp.bitwise_xor(lax.rem(place_ref[0], 8) // 2, flip)
+
+
+def update(place_ref, keep_ref, tile, rows, panel, t, s):
+    wanted = 2 * s + place_ref[1] <= t * place_ref[2] + place_ref[0]
+    kept = jnp.where(keep_ref[t, s] == 1, tile, 0.0)
+    return kept - jnp.where(wanted, product(rows, panel), 0.0)
+
+
+def third_kernel(
+    place_ref, keep_ref, inv0_ref, low_ref, inv1_ref, own_ref, other_ref, at_ref, a_ref, b_ref, tiles_ref,
+    out_ref, rows_ref, hops, tiles, result, sems, hop_sems, out_sems,
 ):
-    p, q = place_ref[0], place_ref[1]
-    edge, count, pairs = tiles_ref.shape[-1], tiles_ref.shape[0], tiles_ref.shape[1]
+    core0 = place_ref[1] == 0
+    edge, count = tiles_ref.shape[-1], tiles_ref.shape[0]
     copy = pltpu.make_async_copy
     loads = [
-        copy(own_ref, own, sems.at[0]),
-        copy(other_ref, other, sems.at[1]),
-        copy(tiles_ref, tiles, sems.at[2]),
+        copy(ref, hops.at[i], hop_sems.at[i])
+        for i, ref in enumerate((own_ref, other_ref, at_ref, a_ref, b_ref))
     ]
-    hop_loads = [
-        copy(ref, hops.at[i], hop_sems.at[i]) for i, ref in enumerate((at_ref, a_ref, b_ref, c_ref))
-    ]
-    for load in loads[:2] + hop_loads + loads[2:]:
+    loads.append(copy(tiles_ref, tiles, sems.at[0]))
+    for load in loads:
         load.start()
+    factors = right6(inv0_ref[...]), right6(low_ref[...]), right6(inv1_ref[...])
     row = lax.broadcasted_iota(jnp.int32, (edge, edge), 0)
     lower = row >= lax.broadcasted_iota(jnp.int32, (edge, edge), 1)
-    inv0, low, inv1 = right6(inv0_ref[...]), right6(low_ref[...]), right6(inv1_ref[...])
-
-    def solve(left, right):
-        first = product(left6(left), inv0)
-        return first, product(left6(right - product(left6(first), low)), inv1)
-
-    for load in loads[:2] + hop_loads:
+    for load in loads:
         load.wait()
-    rows, panels = [], []
+    stores, rows = [], []
     for t in range(count):
-        i = t * place_ref[2] + p
-        first, second = solve(
-            jnp.where(q == 0, own[t], other[t]), jnp.where(q == 0, other[t], own[t])
-        )
+        i = t * place_ref[2] + place_ref[0]
+        left = jnp.where(core0, hops[0, t], hops[1, t])
+        first, second = solve(left, jnp.where(core0, hops[1, t], hops[0, t]), *factors)
         first = jnp.where((i > 0) | lower, first, 0.0)
         second = jnp.where((i > 1) | ((i == 1) & lower), second, 0.0)
-        result[t, 0] = jnp.where(q == 0, first, second)
+        result[t, 3] = jnp.where(core0, first, second)
+        rows_ref[t, :, :edge] = first
+        rows_ref[t, :, edge:] = second
         rows.append(left3(jnp.concatenate([first, second], 1)))
-    for i in range(4):
-        first, second = solve(
-            jnp.where(q == 0, hops[i, 0], hops[i, 1]), jnp.where(q == 0, hops[i, 1], hops[i, 0])
-        )
-        panels.append(right3(jnp.concatenate([first, second], 1)))
-    loads[2].wait()
-    for i in range(4):
-        flip = jnp.where(q == 0, i, (i % 2) * 2 + i // 2)
-        s = jnp.bitwise_xor(lax.rem(p, 8) // 2, flip)
-        room = jnp.where(s > 0, s, pairs)
+        stores.append(copy(result.at[t, 3], out_ref.at[t, 0], out_sems.at[t, 3]))
+    panels = []
+    for i in range(3):
+        left = jnp.where(core0, hops[i + 2, 0], hops[i + 2, 1])
+        both = solve(left, jnp.where(core0, hops[i + 2, 1], hops[i + 2, 0]), *factors)
+        panels.append(right3(jnp.concatenate(both, 1)))
+    for i in range(3):
+        s = slot_of(place_ref, i)
         for t in range(count):
-            wanted = 2 * s + q <= t * place_ref[2] + p
-            tile = jnp.where(keep_ref[t, s] == 1, tiles[t, s], 0.0)
-            result[t, room] = tile - jnp.where(wanted, product(rows[t], panels[i]), 0.0)
-
-    for t in range(count):
-        copy(result.at[t, pl.ds(0, pairs)], out_ref.at[t], out_sems.at[t]).start()
-    for t in range(count):
-        copy(result.at[t, pl.ds(0, pairs)], out_ref.at[t], out_sems.at[t]).wait()
-
-
-def call(kernel, name, outs, specs, scratch, flops, *args, out_specs=VMEM):
+            result[t, i] = update(place_ref, keep_ref, tiles[t, s], rows[t], panels[i], t, s)
+    for store in stores:
+        store.start()
+    for i in range(3):
+        s = slot_of(place_ref, i)
+
+        @pl.when(s > 0)
+        def _():
+            for t in range(count):
+                copy(result.at[t, i], out_ref.at[t, s], out_sems.at[t, i]).start()
+            for t in range(count):
+                copy(result.at[t, i], out_ref.at[t, s], out_sems.at[t, i]).wait()
+
+    for store in stores:
+        store.wait()
+
+
+def fourth_kernel(
+    place_ref, keep_ref, inv0_ref, low_ref, inv1_ref, rows_ref, c_ref, tiles_ref, _,
+    out_ref, tiles, result, sems, out_sems,
+):
+    s = slot_of(place_ref, 3)
+
+    @pl.when(s > 0)
+    def _():
+        core0 = place_ref[1] == 0
+        count = tiles.shape[0]
+        copy = pltpu.make_async_copy
+        loads = [copy(tiles_ref.at[t, s], tiles.at[t], sems.at[t]) for t in range(count)]
+        stores = [copy(result.at[t], out_ref.at[t, s], out_sems.at[t]) for t in range(count)]
+        for load in loads:
+            load.start()
+        factors = right6(inv0_ref[...]), right6(low_ref[...]), right6(inv1_ref[...])
+        both = solve(jnp.where(core0, c_ref[0], c_ref[1]), jnp.where(core0, c_ref[1], c_ref[0]), *factors)
+        panel = right3(jnp.concatenate(both, 1))
+        rows = [left3(rows_ref[t]) for t in range(count)]
+        for load in loads:
+            load.wait()
+        for t in range(count):
+            result[t] = update(place_ref, keep_ref, tiles[t], rows[t], panel, t, s)
+            stores[t].start()
+        for store in stores:
+            store.wait()
+
+
+def call(kernel, name, outs, specs, scratch, flops, *args, out_specs=VMEM, aliases={}):
     return pl.pallas_call(
         kernel,
         out_shape=outs,
         in_specs=specs,
         out_specs=out_specs,
+        input_output_aliases=aliases,
         scratch_shapes=scratch,
         name=name,
         cost_estimate=pl.CostEstimate(flops=flops, bytes_accessed=1 << 20, transcendentals=0),
@@ -312,20 +355,29 @@
     rc = send(ra, [(i, c, i ^ flips[1 - c], c) for i in range(n) for c in range(2)])
     own = jnp.stack([mine, jnp.where(keep[1, 0] == 1, matrix[1, 0, 0, 0], 0.0)])
     other = send(after(own, inv1), [(i, c, i, 1 - c) for i in range(n) for c in range(2)])
+    three, five = pltpu.SemaphoreType.DMA((3,)), pltpu.SemaphoreType.DMA((5,))
+    out, rows = call(
+        third_kernel, "third",
+        [
+            jax.ShapeDtypeStruct(tiles.shape, F32),
+            jax.ShapeDtypeStruct((row_count, edge, 2 * edge), F32),
+        ],
+        [SMEM, SMEM] + [VMEM] * 3 + [ANY] * 6,
+        [
+            pltpu.VMEM((5,) + at.shape, F32),
+            pltpu.VMEM(tiles.shape, F32),
+            pltpu.VMEM((row_count, 4, edge, edge), F32),
+            three,
+            five,
+            pltpu.SemaphoreType.DMA((row_count, 4)),
+        ],
+        10**10, place, keep, inv0, low, inv1, own, other, at, ra, rb, tiles, out_specs=[ANY, VMEM],
+    )
     out = call(
-        last_kernel, "last", jax.ShapeDtypeStruct(tiles.shape, F32),
-        [SMEM, SMEM, VMEM, VMEM, VMEM] + [ANY] * 7,
-        [
-            pltpu.VMEM(own.shape, F32),
-            pltpu.VMEM(own.shape, F32),
-            pltpu.VMEM((4,) + at.shape, F32),
-            pltpu.VMEM(tiles.shape, F32),
-            pltpu.VMEM((row_count, pair_count + 1, edge, edge), F32),
-            pltpu.SemaphoreType.DMA((3,)),
-            pltpu.SemaphoreType.DMA((4,)),
-            pltpu.SemaphoreType.DMA((row_count,)),
-        ],
-        10**10, place, keep, inv0, low, inv1, own, other, at, ra, rb, rc, tiles, out_specs=ANY,
+        fourth_kernel, "fourth", jax.ShapeDtypeStruct(tiles.shape, F32),
+        [SMEM, SMEM] + [VMEM] * 5 + [ANY] * 2,
+        [pltpu.VMEM(own.shape, F32), pltpu.VMEM(own.shape, F32), three, three],
+        10**10, place, keep, inv0, low, inv1, rows, rc, tiles, out, out_specs=ANY, aliases={8: 0},
     )
     return out[:, None, :, None]
 

time: 71.8 us -> 69.2 us (0.964)
  waiting for transfers between devices: 29.2 us -> 24.8 us
  Pallas kernels: 18.8 us -> 22.2 us
  starting transfers between devices: 18.3 us -> 17.4 us
    ppermute x14, waiting for transfers between devices: 29.2 us -> 24.8 us  [send(): lax.ppermute(x, ('row', 'col'), [(2 * a + b, 2 * c + d) for a, b, c, d in...]
    pallas_call x3 -> x4, Pallas kernels: 18.8 us -> 22.2 us  [call(): pl.pallas_call(kernel, out_shape=outs, in_specs=specs, out_specs=out_spec...]
    ppermute x14, starting transfers between devices: 18.3 us -> 17.4 us  [send(): lax.ppermute(x, ('row', 'col'), [(2 * a + b, 2 * c + d) for a, b, c, d in...]
  transfers between devices with their start and end apart: 14 -> 14, of which waited for: 5 -> 4; matrix products, arithmetic and copies ran while one was open for 1% -> 1% of each run, Pallas kernels for 11% -> 26%
where the time goes in v4:
time: 69.2 us; the launch traced here: 68.9 us
  waiting for transfers between devices  24.8 us (36%)
  Pallas kernels  22.2 us (32%)
  starting transfers between devices  17.4 us (25%)
  other arithmetic  2.32 us (3%)
  between operations  1.7 us (2%)
    ppermute x14, waiting for transfers between devices, send(): lax.ppermute(x, ('row', 'col'), [(2 * a + b, 2 * c + d) for a, b, c, d in...  24.8 us
    pallas_call x4, Pallas kernels, call(): pl.pallas_call(kernel, out_shape=outs, in_specs=specs, out_specs=out_spec...  22.2 us
    ppermute x14, starting transfers between devices, send(): lax.ppermute(x, ('row', 'col'), [(2 * a + b, 2 * c + d) for a, b, c, d in...  17.4 us
  transfers between devices with their start and end apart: 14, of which 4 were waited for; matrix products, arithmetic and copies ran while one was open for 1% of the time, Pallas kernels for 26%

profile of v4, /device:TPU:25, one launch (start us, length us, event | category | flops | bytes accessed | tf_op | source)
XLA Modules:
  0.0 68.9 jit_solution(9893293426642835837)
XLA Ops:
  0.0 0.7 broadcast_compare_fusion
  0.7 0.1 fusion.5.keep_ref
  0.8 0.6 fusion.6
  2.6 1.1 %fusion = (f32[1,256,256]{2,1,0:T(8,128)S(1)}, f32[256,256]{1,0:T(8,128)S(1)}, f32[1,256,256]{2,1,0:T(8,128)S(1)}) fusion(f32[2,1,4,1,256,256]{5,4,3,2,1,0:T(8,128)} %param.2, pred[]{:T(512)} %bitcast.2, pred[]{:T(512)} %bitcast.9), kind=kLoop, calls=%fused_computation.9 | loop fusion | flops 131072 | bytes 1310722 | tf_op jit(solution)/shard_map/jit(_where)/select_n | solution.py:303
  3.7 0.1 pad_add_fusion.place_ref
  3.8 0.6 first.1
  4.3 0.7 collective-permute-start
  5.0 0.7 collective-permute-start.1
  5.7 0.7 collective-permute-start.2
  6.4 1.3 %collective-permute-start.6 = (f32[256,256]{1,0:T(8,128)S(1)}, f32[256,256]{1,0:T(8,128)S(1)}, u32[]{:S(2)}, u32[]{:S(2)}) collective-permute-start(f32[256,256]{1,0:T(8,128)S(1)} %get-tuple-element.22.tile_ref), channel_id=1, source_target_pairs={{4,20},{5,21},{6,22},{7,23},{8,24},{9,25},{10,26},{11,27},{12,28},... | collective-permute-start | bytes 786440 | tf_op jit(solution)/shard_map/ppermute | solution.py:301
  7.7 0.0 collective-permute-done
  7.7 0.0 collective-permute-done.1
  7.8 0.0 collective-permute-done.2
  7.8 0.1 select_select_fusion
  7.9 0.7 collective-permute-start.3
  8.5 0.7 collective-permute-start.4
  9.2 1.3 %collective-permute-start.5 = (f32[256,256]{1,0:T(8,128)S(1)}, f32[256,256]{1,0:T(8,128)S(1)}, u32[]{:S(2)}, u32[]{:S(2)}) collective-permute-start(f32[256,256]{1,0:T(8,128)S(1)} %select_select_fusion), channel_id=1, source_target_pairs={{0,10},{2,8},{3,9},{4,14},{6,12},{7,13},{16,26},{18,24},{19,25},{2... | collective-permute-start | bytes 786440 | tf_op jit(solution)/shard_map/ppermute | solution.py:301
  10.5 12.0 %collective-permute-done.6 = f32[256,256]{1,0:T(8,128)S(1)} collective-permute-done((f32[256,256]{1,0:T(8,128)S(1)}, f32[256,256]{1,0:T(8,128)S(1)}, u32[]{:S(2)}, u32[]{:S(2)}) %collective-permute-start.6) | collective-permute-done | bytes 262176 | tf_op jit(solution)/shard_map/ppermute | solution.py:301
  22.6 3.0 %collective-permute-start.7 = (f32[256,256]{1,0:T(8,128)S(1)}, f32[256,256]{1,0:T(8,128)S(1)}, u32[]{:S(2)}, u32[]{:S(2)}) collective-permute-start(f32[256,256]{1,0:T(8,128)S(1)} %broadcast_select_fusion), channel_id=1, source_target_pairs={{4,6},{7,5},{8,10},{11,9},{12,14},{15,13},{20,22},{23,21},{24,26},... | collective-permute-start | bytes 786440 | tf_op jit(solution)/shard_map/ppermute | solution.py:301
  25.6 7.6 %collective-permute-start.8 = (f32[256,256]{1,0:T(8,128)S(1)}, f32[256,256]{1,0:T(8,128)S(1)}, u32[]{:S(2)}, u32[]{:S(2)}) collective-permute-start(f32[256,256]{1,0:T(8,128)S(1)} %broadcast_select_fusion), channel_id=1, source_target_pairs={{5,6},{6,5},{9,10},{10,9},{13,14},{14,13},{21,22},{22,21},{25,26},... | collective-permute-start | bytes 786440 | tf_op jit(solution)/shard_map/ppermute | solution.py:301
  33.2 0.0 collective-permute-done.3
  33.2 0.0 collective-permute-done.4
  33.2 6.4 %collective-permute-done.5 = f32[256,256]{1,0:T(8,128)S(1)} collective-permute-done((f32[256,256]{1,0:T(8,128)S(1)}, f32[256,256]{1,0:T(8,128)S(1)}, u32[]{:S(2)}, u32[]{:S(2)}) %collective-permute-start.5) | collective-permute-done | bytes 262176 | tf_op jit(solution)/shard_map/ppermute | solution.py:301
  39.7 0.1 select_bitcast_fusion.3
  39.8 0.6 collective-permute-start.9
  40.5 0.0 collective-permute-done.7
  40.5 2.4 %collective-permute-done.8 = f32[256,256]{1,0:T(8,128)S(1)} collective-permute-done((f32[256,256]{1,0:T(8,128)S(1)}, f32[256,256]{1,0:T(8,128)S(1)}, u32[]{:S(2)}, u32[]{:S(2)}) %collective-permute-start.8) | collective-permute-done | bytes 262176 | tf_op jit(solution)/shard_map/ppermute | solution.py:301
  42.8 0.1 select_bitcast_fusion.2
  42.9 0.1 collective-permute-start.11
  43.0 0.1 collective-permute-start.12
  43.1 0.0 collective-permute-done.9.other_ref
  43.1 7.8 %second.1 = (f32[256,256]{1,0:T(8,128)S(1)}, f32[256,256]{1,0:T(8,128)S(1)}, f32[256,256]{1,0:T(8,128)S(1)}) custom-call(s32[3]{0:T(128)S(1)} %pad_add_fusion.place_ref, f32[2,256,256]{2,1,0:T(8,128)S(1)} %pad_maximum_fusion.own_ref, f32[2,256,256]{2,1,0:T(8,128)S(1)} %collective-permute-done.9.other_ref), custom_call_target="tpu_custom_call" | custom-call | flops 10000000000 | bytes 1048576 | tf_op jit(solution)/shard_map/second/pallas_call | solution.py:269
  50.9 0.1 collective-permute-start.10
  51.0 3.9 %collective-permute-done.11.a_ref = f32[2,256,256]{2,1,0:T(8,128)S(1)} collective-permute-done((f32[2,256,256]{2,1,0:T(8,128)S(1)}, f32[2,256,256]{2,1,0:T(8,128)S(1)}, u32[]{:S(2)}, u32[]{:S(2)}) %collective-permute-start.11) | collective-permute-done | bytes 524320 | tf_op jit(solution)/shard_map/ppermute | solution.py:301
  54.9 0.0 collective-permute-start.13
  54.9 0.0 collective-permute-done.12.b_ref
  54.9 0.0 collective-permute-done.10.other_ref
  54.9 0.0 copy-start
  54.9 10.3 %third.1 = (f32[2,4,256,256]{3,2,1,0:T(8,128)}, f32[2,256,512]{2,1,0:T(8,128)S(1)}) custom-call(s32[3]{0:T(128)S(1)} %pad_add_fusion.place_ref, s32[2,4]{1,0:T(2,128)S(1)} %fusion.5.keep_ref, f32[256,256]{1,0:T(8,128)S(1)} %get-tuple-element.14.inv0_ref, f32[256,256]{1,0:T(8,128)S(1)} %get-tuple-element.15.low_ref, ...), custom_call_target="tpu_custom_call" | custom-call | flops 10000000000 | bytes 1048576 | tf_op jit(solution)/shard_map/third/pallas_call | solution.py:269
  65.2 0.0 collective-permute-done.13.c_ref
  65.2 0.0 copy-done
  65.2 3.5 %fourth.1 = f32[2,4,256,256]{3,2,1,0:T(8,128)} custom-call(s32[3]{0:T(128)S(1)} %pad_add_fusion.place_ref, s32[2,4]{1,0:T(2,128)S(1)} %fusion.5.keep_ref, f32[256,256]{1,0:T(8,128)S(1)} %get-tuple-element.14.inv0_ref, f32[256,256]{1,0:T(8,128)S(1)} %get-tuple-element.15.low_ref, ...), custom_call_target="tpu_custom_call", output_to_operand_aliasing={{}: (8, {})} | custom-call | flops 10000000000 | bytes 1048576 | tf_op jit(solution)/shard_map/fourth/pallas_call | solution.py:269
  (6 shorter events, 0.1 us)
Async XLA Ops:
  4.3 3.4 %collective-permute-start = (f32[256,256]{1,0:T(8,128)S(1)}, f32[256,256]{1,0:T(8,128)S(1)}, u32[]{:S(2)}, u32[]{:S(2)}) collective-permute-start(f32[256,256]{1,0:T(8,128)S(1)} %first.1), channel_id=1, source_target_pairs={{0,20},{2,22},{3,23}} | collective-permute-start | bytes 786440 | tf_op jit(solution)/shard_map/ppermute | solution.py:301
  5.0 2.7 %collective-permute-start.1 = (f32[256,256]{1,0:T(8,128)S(1)}, f32[256,256]{1,0:T(8,128)S(1)}, u32[]{:S(2)}, u32[]{:S(2)}) collective-permute-start(f32[256,256]{1,0:T(8,128)S(1)} %first.1), channel_id=1, source_target_pairs={{0,16},{2,18},{3,19}} | collective-permute-start | bytes 786440 | tf_op jit(solution)/shard_map/ppermute | solution.py:301
  5.7 2.0 %collective-permute-start.2 = (f32[256,256]{1,0:T(8,128)S(1)}, f32[256,256]{1,0:T(8,128)S(1)}, u32[]{:S(2)}, u32[]{:S(2)}) collective-permute-start(f32[256,256]{1,0:T(8,128)S(1)} %first.1), channel_id=1, source_target_pairs={{0,4},{2,6},{3,7}} | collective-permute-start | bytes 786440 | tf_op jit(solution)/shard_map/ppermute | solution.py:301
  6.4 16.2 %collective-permute-start.6 = (f32[256,256]{1,0:T(8,128)S(1)}, f32[256,256]{1,0:T(8,128)S(1)}, u32[]{:S(2)}, u32[]{:S(2)}) collective-permute-start(f32[256,256]{1,0:T(8,128)S(1)} %get-tuple-element.22.tile_ref), channel_id=1, source_target_pairs={{4,20},{5,21},{6,22},{7,23},{8,24},{9,25},{10,26},{11,27},{12,28},... | collective-permute-start | bytes 786440 | tf_op jit(solution)/shard_map/ppermute | solution.py:301
  7.9 25.3 %collective-permute-start.3 = (f32[256,256]{1,0:T(8,128)S(1)}, f32[256,256]{1,0:T(8,128)S(1)}, u32[]{:S(2)}, u32[]{:S(2)}) collective-permute-start(f32[256,256]{1,0:T(8,128)S(1)} %select_select_fusion), channel_id=1, source_target_pairs={{0,8},{2,10},{3,11},{4,12},{6,14},{7,15},{16,24},{18,26},{19,27},{... | collective-permute-start | bytes 786440 | tf_op jit(solution)/shard_map/ppermute | solution.py:301
  8.5 24.7 %collective-permute-start.4 = (f32[256,256]{1,0:T(8,128)S(1)}, f32[256,256]{1,0:T(8,128)S(1)}, u32[]{:S(2)}, u32[]{:S(2)}) collective-permute-start(f32[256,256]{1,0:T(8,128)S(1)} %select_select_fusion), channel_id=1, source_target_pairs={{0,2},{2,0},{3,1},{4,6},{6,4},{7,5},{16,18},{18,16},{19,17},{20,22... | collective-permute-start | bytes 786440 | tf_op jit(solution)/shard_map/ppermute | solution.py:301
  9.2 30.4 %collective-permute-start.5 = (f32[256,256]{1,0:T(8,128)S(1)}, f32[256,256]{1,0:T(8,128)S(1)}, u32[]{:S(2)}, u32[]{:S(2)}) collective-permute-start(f32[256,256]{1,0:T(8,128)S(1)} %select_select_fusion), channel_id=1, source_target_pairs={{0,10},{2,8},{3,9},{4,14},{6,12},{7,13},{16,26},{18,24},{19,25},{2... | collective-permute-start | bytes 786440 | tf_op jit(solution)/shard_map/ppermute | solution.py:301
  22.6 17.8 %collective-permute-start.7 = (f32[256,256]{1,0:T(8,128)S(1)}, f32[256,256]{1,0:T(8,128)S(1)}, u32[]{:S(2)}, u32[]{:S(2)}) collective-permute-start(f32[256,256]{1,0:T(8,128)S(1)} %broadcast_select_fusion), channel_id=1, source_target_pairs={{4,6},{7,5},{8,10},{11,9},{12,14},{15,13},{20,22},{23,21},{24,26},... | collective-permute-start | bytes 786440 | tf_op jit(solution)/shard_map/ppermute | solution.py:301
  25.6 17.2 %collective-permute-start.8 = (f32[256,256]{1,0:T(8,128)S(1)}, f32[256,256]{1,0:T(8,128)S(1)}, u32[]{:S(2)}, u32[]{:S(2)}) collective-permute-start(f32[256,256]{1,0:T(8,128)S(1)} %broadcast_select_fusion), channel_id=1, source_target_pairs={{5,6},{6,5},{9,10},{10,9},{13,14},{14,13},{21,22},{22,21},{25,26},... | collective-permute-start | bytes 786440 | tf_op jit(solution)/shard_map/ppermute | solution.py:301
  39.8 3.3 %collective-permute-start.9 = (f32[2,256,256]{2,1,0:T(8,128)S(1)}, f32[2,256,256]{2,1,0:T(8,128)S(1)}, u32[]{:S(2)}, u32[]{:S(2)}) collective-permute-start(f32[2,256,256]{2,1,0:T(8,128)S(1)} %pad_maximum_fusion.own_ref), channel_id=1, source_target_pairs={{0,1},{1,0},{2,3},{3,2},{4,5},{5,4},{6,7},{7,6},{8,9},{9,8},{10,11... | collective-permute-start | bytes 1572872 | tf_op jit(solution)/shard_map/ppermute | solution.py:301
  42.9 11.9 %collective-permute-start.11 = (f32[2,256,256]{2,1,0:T(8,128)S(1)}, f32[2,256,256]{2,1,0:T(8,128)S(1)}, u32[]{:S(2)}, u32[]{:S(2)}) collective-permute-start(f32[2,256,256]{2,1,0:T(8,128)S(1)} %pad_maximum_fusion.1.at_ref), channel_id=1, source_target_pairs={{0,4},{1,9},{2,6},{3,11},{4,0},{5,13},{6,2},{7,15},{8,12},{9,1},{1... | collective-permute-start | bytes 1572872 | tf_op jit(solution)/shard_map/ppermute | solution.py:301
  43.0 11.9 %collective-permute-start.12 = (f32[2,256,256]{2,1,0:T(8,128)S(1)}, f32[2,256,256]{2,1,0:T(8,128)S(1)}, u32[]{:S(2)}, u32[]{:S(2)}) collective-permute-start(f32[2,256,256]{2,1,0:T(8,128)S(1)} %pad_maximum_fusion.1.at_ref), channel_id=1, source_target_pairs={{0,8},{1,5},{2,10},{3,7},{4,12},{5,1},{6,14},{7,3},{8,0},{9,13},{1... | collective-permute-start | bytes 1572872 | tf_op jit(solution)/shard_map/ppermute | solution.py:301
  50.9 4.0 %collective-permute-start.10 = (f32[2,256,256]{2,1,0:T(8,128)S(1)}, f32[2,256,256]{2,1,0:T(8,128)S(1)}, u32[]{:S(2)}, u32[]{:S(2)}) collective-permute-start(f32[2,256,256]{2,1,0:T(8,128)S(1)} %pad_maximum_fusion.2.own_ref), channel_id=1, source_target_pairs={{0,1},{1,0},{2,3},{3,2},{4,5},{5,4},{6,7},{7,6},{8,9},{9,8},{10,11... | collective-permute-start | bytes 1572872 | tf_op jit(solution)/shard_map/ppermute | solution.py:301
  54.9 10.3 %collective-permute-start.13 = (f32[2,256,256]{2,1,0:T(8,128)S(1)}, f32[2,256,256]{2,1,0:T(8,128)S(1)}, u32[]{:S(2)}, u32[]{:S(2)}) collective-permute-start(f32[2,256,256]{2,1,0:T(8,128)S(1)} %collective-permute-done.11.a_ref), channel_id=1, source_target_pairs={{0,8},{1,5},{2,10},{3,7},{4,12},{5,1},{6,14},{7,3},{8,0},{9,13},{1... | collective-permute-start | bytes 1572872 | tf_op jit(solution)/shard_map/ppermute | solution.py:301
  54.9 10.3 %copy-start = (f32[2,1,4,1,256,256]{5,4,3,2,1,0:T(8,128)S(1)}, f32[2,1,4,1,256,256]{5,4,3,2,1,0:T(8,128)}, u32[]{:S(2)}) copy-start(f32[2,1,4,1,256,256]{5,4,3,2,1,0:T(8,128)} %param.2) | copy-start | bytes 6291460

commit v5 on v4

--- a/solution.py
+++ b/solution.py
@@ -198,13 +198,21 @@
     factors = right6(inv0_ref[...]), right6(low_ref[...]), right6(inv1_ref[...])
     row = lax.broadcasted_iota(jnp.int32, (edge, edge), 0)
     lower = row >= lax.broadcasted_iota(jnp.int32, (edge, edge), 1)
-    for load in loads:
+    for load in loads[:5]:
         load.wait()
+    lefts = [jnp.where(core0, hops[0, t], hops[1, t]) for t in range(count)]
+    rights = [jnp.where(core0, hops[1, t], hops[0, t]) for t in range(count)]
+    for i in range(2, 5):
+        lefts.append(jnp.where(core0, hops[i, 0], hops[i, 1]))
+        rights.append(jnp.where(core0, hops[i, 1], hops[i, 0]))
+    inv0, low, inv1 = factors
+    firsts = [product(left6(x), inv0) for x in lefts]
+    rests = [x - product(left6(first), low) for x, first in zip(rights, firsts)]
+    seconds = [product(left6(x), inv1) for x in rests]
     stores, rows = [], []
     for t in range(count):
         i = t * place_ref[2] + place_ref[0]
-        left = jnp.where(core0, hops[0, t], hops[1, t])
-        first, second = solve(left, jnp.where(core0, hops[1, t], hops[0, t]), *factors)
+        first, second = firsts[t], seconds[t]
         first = jnp.where((i > 0) | lower, first, 0.0)
         second = jnp.where((i > 1) | ((i == 1) & lower), second, 0.0)
         result[t, 3] = jnp.where(core0, first, second)
@@ -212,11 +220,8 @@
         rows_ref[t, :, edge:] = second
         rows.append(left3(jnp.concatenate([first, second], 1)))
         stores.append(copy(result.at[t, 3], out_ref.at[t, 0], out_sems.at[t, 3]))
-    panels = []
-    for i in range(3):
-        left = jnp.where(core0, hops[i + 2, 0], hops[i + 2, 1])
-        both = solve(left, jnp.where(core0, hops[i + 2, 1], hops[i + 2, 0]), *factors)
-        panels.append(right3(jnp.concatenate(both, 1)))
+    panels = [right3(jnp.concatenate(both, 1)) for both in zip(firsts[count:], seconds[count:])]
+    loads[5].wait()
     for i in range(3):
         s = slot_of(place_ref, i)
         for t in range(count):

time: 69.2 us -> 66.9 us (0.967)
  Pallas kernels: 22.2 us -> 19.6 us
    pallas_call x4, Pallas kernels: 22.2 us -> 19.6 us  [call(): pl.pallas_call(kernel, out_shape=outs, in_specs=specs, out_specs=out_spec...]
  transfers between devices with their start and end apart: 14 -> 14, of which waited for: 4 -> 5; matrix products, arithmetic and copies ran while one was open for 1% -> 1% of each run, Pallas kernels for 26% -> 23%
where the time goes in v5:
time: 66.9 us; the launch traced here: 66.6 us
  waiting for transfers between devices  25.1 us (38%)
  Pallas kernels  19.6 us (29%)
  starting transfers between devices  17.4 us (26%)
  other arithmetic  2.32 us (3%)
  between operations  1.68 us (3%)
    ppermute x14, waiting for transfers between devices, send(): lax.ppermute(x, ('row', 'col'), [(2 * a + b, 2 * c + d) for a, b, c, d in...  25.1 us
    pallas_call x4, Pallas kernels, call(): pl.pallas_call(kernel, out_shape=outs, in_specs=specs, out_specs=out_spec...  19.6 us
    ppermute x14, starting transfers between devices, send(): lax.ppermute(x, ('row', 'col'), [(2 * a + b, 2 * c + d) for a, b, c, d in...  17.4 us
  transfers between devices with their start and end apart: 14, of which 5 were waited for; matrix products, arithmetic and copies ran while one was open for 1% of the time, Pallas kernels for 23%

profile of v5, /device:TPU:25, one launch (start us, length us, event | category | flops | bytes accessed | tf_op | source)
XLA Modules:
  0.0 66.6 jit_solution(3553157647663648810)
XLA Ops:
  0.0 0.7 %broadcast_compare_fusion = pred[2,1,4,1]{2,3,1,0:T(4,128)(4,1)S(1)} fusion(s32[2,1,4,1]{2,3,1,0:T(1,128)} %param.3), kind=kLoop, calls=%fused_computation.23 | loop fusion | flops 8 | bytes 40 | tf_op jit(solution)/shard_map/eq | solution.py:299
  0.7 0.1 fusion.5.keep_ref
  0.8 0.6 fusion.6
  2.6 1.1 %fusion = (f32[1,256,256]{2,1,0:T(8,128)S(1)}, f32[256,256]{1,0:T(8,128)S(1)}, f32[1,256,256]{2,1,0:T(8,128)S(1)}) fusion(f32[2,1,4,1,256,256]{5,4,3,2,1,0:T(8,128)} %param.2, pred[]{:T(512)} %bitcast.2, pred[]{:T(512)} %bitcast.9), kind=kLoop, calls=%fused_computation.9 | loop fusion | flops 131072 | bytes 1310722 | tf_op jit(solution)/shard_map/jit(_where)/select_n | solution.py:308
  3.7 0.1 pad_add_fusion.place_ref
  3.8 0.6 first.1
  4.3 0.7 %collective-permute-start = (f32[256,256]{1,0:T(8,128)S(1)}, f32[256,256]{1,0:T(8,128)S(1)}, u32[]{:S(2)}, u32[]{:S(2)}) collective-permute-start(f32[256,256]{1,0:T(8,128)S(1)} %first.1), channel_id=1, source_target_pairs={{0,20},{2,22},{3,23}} | collective-permute-start | bytes 786440 | tf_op jit(solution)/shard_map/ppermute | solution.py:306
  5.0 0.7 %collective-permute-start.1 = (f32[256,256]{1,0:T(8,128)S(1)}, f32[256,256]{1,0:T(8,128)S(1)}, u32[]{:S(2)}, u32[]{:S(2)}) collective-permute-start(f32[256,256]{1,0:T(8,128)S(1)} %first.1), channel_id=1, source_target_pairs={{0,16},{2,18},{3,19}} | collective-permute-start | bytes 786440 | tf_op jit(solution)/shard_map/ppermute | solution.py:306
  5.7 0.7 %collective-permute-start.2 = (f32[256,256]{1,0:T(8,128)S(1)}, f32[256,256]{1,0:T(8,128)S(1)}, u32[]{:S(2)}, u32[]{:S(2)}) collective-permute-start(f32[256,256]{1,0:T(8,128)S(1)} %first.1), channel_id=1, source_target_pairs={{0,4},{2,6},{3,7}} | collective-permute-start | bytes 786440 | tf_op jit(solution)/shard_map/ppermute | solution.py:306
  6.4 1.3 %collective-permute-start.6 = (f32[256,256]{1,0:T(8,128)S(1)}, f32[256,256]{1,0:T(8,128)S(1)}, u32[]{:S(2)}, u32[]{:S(2)}) collective-permute-start(f32[256,256]{1,0:T(8,128)S(1)} %get-tuple-element.22.tile_ref), channel_id=1, source_target_pairs={{4,20},{5,21},{6,22},{7,23},{8,24},{9,25},{10,26},{11,27},{12,28},... | collective-permute-start | bytes 786440 | tf_op jit(solution)/shard_map/ppermute | solution.py:306
  7.7 0.0 collective-permute-done
  7.7 0.0 collective-permute-done.1
  7.8 0.0 collective-permute-done.2
  7.8 0.1 select_select_fusion
  7.9 0.7 %collective-permute-start.3 = (f32[256,256]{1,0:T(8,128)S(1)}, f32[256,256]{1,0:T(8,128)S(1)}, u32[]{:S(2)}, u32[]{:S(2)}) collective-permute-start(f32[256,256]{1,0:T(8,128)S(1)} %select_select_fusion), channel_id=1, source_target_pairs={{0,8},{2,10},{3,11},{4,12},{6,14},{7,15},{16,24},{18,26},{19,27},{... | collective-permute-start | bytes 786440 | tf_op jit(solution)/shard_map/ppermute | solution.py:306
  8.5 0.7 %collective-permute-start.4 = (f32[256,256]{1,0:T(8,128)S(1)}, f32[256,256]{1,0:T(8,128)S(1)}, u32[]{:S(2)}, u32[]{:S(2)}) collective-permute-start(f32[256,256]{1,0:T(8,128)S(1)} %select_select_fusion), channel_id=1, source_target_pairs={{0,2},{2,0},{3,1},{4,6},{6,4},{7,5},{16,18},{18,16},{19,17},{20,22... | collective-permute-start | bytes 786440 | tf_op jit(solution)/shard_map/ppermute | solution.py:306
  9.2 1.3 %collective-permute-start.5 = (f32[256,256]{1,0:T(8,128)S(1)}, f32[256,256]{1,0:T(8,128)S(1)}, u32[]{:S(2)}, u32[]{:S(2)}) collective-permute-start(f32[256,256]{1,0:T(8,128)S(1)} %select_select_fusion), channel_id=1, source_target_pairs={{0,10},{2,8},{3,9},{4,14},{6,12},{7,13},{16,26},{18,24},{19,25},{2... | collective-permute-start | bytes 786440 | tf_op jit(solution)/shard_map/ppermute | solution.py:306
  10.5 12.0 %collective-permute-done.6 = f32[256,256]{1,0:T(8,128)S(1)} collective-permute-done((f32[256,256]{1,0:T(8,128)S(1)}, f32[256,256]{1,0:T(8,128)S(1)}, u32[]{:S(2)}, u32[]{:S(2)}) %collective-permute-start.6) | collective-permute-done | bytes 262176 | tf_op jit(solution)/shard_map/ppermute | solution.py:306
  22.6 3.0 %collective-permute-start.7 = (f32[256,256]{1,0:T(8,128)S(1)}, f32[256,256]{1,0:T(8,128)S(1)}, u32[]{:S(2)}, u32[]{:S(2)}) collective-permute-start(f32[256,256]{1,0:T(8,128)S(1)} %broadcast_select_fusion), channel_id=1, source_target_pairs={{4,6},{7,5},{8,10},{11,9},{12,14},{15,13},{20,22},{23,21},{24,26},... | collective-permute-start | bytes 786440 | tf_op jit(solution)/shard_map/ppermute | solution.py:306
  25.6 7.6 %collective-permute-start.8 = (f32[256,256]{1,0:T(8,128)S(1)}, f32[256,256]{1,0:T(8,128)S(1)}, u32[]{:S(2)}, u32[]{:S(2)}) collective-permute-start(f32[256,256]{1,0:T(8,128)S(1)} %broadcast_select_fusion), channel_id=1, source_target_pairs={{5,6},{6,5},{9,10},{10,9},{13,14},{14,13},{21,22},{22,21},{25,26},... | collective-permute-start | bytes 786440 | tf_op jit(solution)/shard_map/ppermute | solution.py:306
  33.2 0.0 collective-permute-done.3
  33.2 0.0 collective-permute-done.4
  33.2 6.4 %collective-permute-done.5 = f32[256,256]{1,0:T(8,128)S(1)} collective-permute-done((f32[256,256]{1,0:T(8,128)S(1)}, f32[256,256]{1,0:T(8,128)S(1)}, u32[]{:S(2)}, u32[]{:S(2)}) %collective-permute-start.5) | collective-permute-done | bytes 262176 | tf_op jit(solution)/shard_map/ppermute | solution.py:306
  39.7 0.1 select_bitcast_fusion.3
  39.8 0.6 collective-permute-start.9
  40.5 0.0 collective-permute-done.7
  40.5 2.4 %collective-permute-done.8 = f32[256,256]{1,0:T(8,128)S(1)} collective-permute-done((f32[256,256]{1,0:T(8,128)S(1)}, f32[256,256]{1,0:T(8,128)S(1)}, u32[]{:S(2)}, u32[]{:S(2)}) %collective-permute-start.8) | collective-permute-done | bytes 262176 | tf_op jit(solution)/shard_map/ppermute | solution.py:306
  42.8 0.1 select_bitcast_fusion.2
  42.9 0.1 collective-permute-start.11
  43.0 0.1 collective-permute-start.12
  43.1 0.0 collective-permute-done.9.other_ref
  43.1 7.8 %second.1 = (f32[256,256]{1,0:T(8,128)S(1)}, f32[256,256]{1,0:T(8,128)S(1)}, f32[256,256]{1,0:T(8,128)S(1)}) custom-call(s32[3]{0:T(128)S(1)} %pad_add_fusion.place_ref, f32[2,256,256]{2,1,0:T(8,128)S(1)} %pad_maximum_fusion.own_ref, f32[2,256,256]{2,1,0:T(8,128)S(1)} %collective-permute-done.9.other_ref), custom_call_target="tpu_custom_call" | custom-call | flops 10000000000 | bytes 1048576 | tf_op jit(solution)/shard_map/second/pallas_call | solution.py:274
  50.9 0.1 collective-permute-start.10
  51.0 3.9 %collective-permute-done.11.a_ref = f32[2,256,256]{2,1,0:T(8,128)S(1)} collective-permute-done((f32[2,256,256]{2,1,0:T(8,128)S(1)}, f32[2,256,256]{2,1,0:T(8,128)S(1)}, u32[]{:S(2)}, u32[]{:S(2)}) %collective-permute-start.11) | collective-permute-done | bytes 524320 | tf_op jit(solution)/shard_map/ppermute | solution.py:306
  54.9 0.0 collective-permute-start.13
  54.9 0.0 collective-permute-done.12.b_ref
  54.9 0.0 collective-permute-done.10.other_ref
  54.9 0.0 copy-start
  54.9 7.7 %third.1 = (f32[2,4,256,256]{3,2,1,0:T(8,128)}, f32[2,256,512]{2,1,0:T(8,128)S(1)}) custom-call(s32[3]{0:T(128)S(1)} %pad_add_fusion.place_ref, s32[2,4]{1,0:T(2,128)S(1)} %fusion.5.keep_ref, f32[256,256]{1,0:T(8,128)S(1)} %get-tuple-element.14.inv0_ref, f32[256,256]{1,0:T(8,128)S(1)} %get-tuple-element.15.low_ref, ...), custom_call_target="tpu_custom_call" | custom-call | flops 10000000000 | bytes 1048576 | tf_op jit(solution)/shard_map/third/pallas_call | solution.py:274
  62.6 0.3 collective-permute-done.13.c_ref
  62.9 0.0 copy-done
  62.9 3.5 %fourth.1 = f32[2,4,256,256]{3,2,1,0:T(8,128)} custom-call(s32[3]{0:T(128)S(1)} %pad_add_fusion.place_ref, s32[2,4]{1,0:T(2,128)S(1)} %fusion.5.keep_ref, f32[256,256]{1,0:T(8,128)S(1)} %get-tuple-element.14.inv0_ref, f32[256,256]{1,0:T(8,128)S(1)} %get-tuple-element.15.low_ref, ...), custom_call_target="tpu_custom_call", output_to_operand_aliasing={{}: (8, {})} | custom-call | flops 10000000000 | bytes 1048576 | tf_op jit(solution)/shard_map/fourth/pallas_call | solution.py:274
  (6 shorter events, 0.1 us)
Async XLA Ops:
  4.3 3.4 %collective-permute-start = (f32[256,256]{1,0:T(8,128)S(1)}, f32[256,256]{1,0:T(8,128)S(1)}, u32[]{:S(2)}, u32[]{:S(2)}) collective-permute-start(f32[256,256]{1,0:T(8,128)S(1)} %first.1), channel_id=1, source_target_pairs={{0,20},{2,22},{3,23}} | collective-permute-start | bytes 786440 | tf_op jit(solution)/shard_map/ppermute | solution.py:306
  5.0 2.7 %collective-permute-start.1 = (f32[256,256]{1,0:T(8,128)S(1)}, f32[256,256]{1,0:T(8,128)S(1)}, u32[]{:S(2)}, u32[]{:S(2)}) collective-permute-start(f32[256,256]{1,0:T(8,128)S(1)} %first.1), channel_id=1, source_target_pairs={{0,16},{2,18},{3,19}} | collective-permute-start | bytes 786440 | tf_op jit(solution)/shard_map/ppermute | solution.py:306
  5.7 2.0 %collective-permute-start.2 = (f32[256,256]{1,0:T(8,128)S(1)}, f32[256,256]{1,0:T(8,128)S(1)}, u32[]{:S(2)}, u32[]{:S(2)}) collective-permute-start(f32[256,256]{1,0:T(8,128)S(1)} %first.1), channel_id=1, source_target_pairs={{0,4},{2,6},{3,7}} | collective-permute-start | bytes 786440 | tf_op jit(solution)/shard_map/ppermute | solution.py:306
  6.4 16.2 %collective-permute-start.6 = (f32[256,256]{1,0:T(8,128)S(1)}, f32[256,256]{1,0:T(8,128)S(1)}, u32[]{:S(2)}, u32[]{:S(2)}) collective-permute-start(f32[256,256]{1,0:T(8,128)S(1)} %get-tuple-element.22.tile_ref), channel_id=1, source_target_pairs={{4,20},{5,21},{6,22},{7,23},{8,24},{9,25},{10,26},{11,27},{12,28},... | collective-permute-start | bytes 786440 | tf_op jit(solution)/shard_map/ppermute | solution.py:306
  7.9 25.3 %collective-permute-start.3 = (f32[256,256]{1,0:T(8,128)S(1)}, f32[256,256]{1,0:T(8,128)S(1)}, u32[]{:S(2)}, u32[]{:S(2)}) collective-permute-start(f32[256,256]{1,0:T(8,128)S(1)} %select_select_fusion), channel_id=1, source_target_pairs={{0,8},{2,10},{3,11},{4,12},{6,14},{7,15},{16,24},{18,26},{19,27},{... | collective-permute-start | bytes 786440 | tf_op jit(solution)/shard_map/ppermute | solution.py:306
  8.5 24.7 %collective-permute-start.4 = (f32[256,256]{1,0:T(8,128)S(1)}, f32[256,256]{1,0:T(8,128)S(1)}, u32[]{:S(2)}, u32[]{:S(2)}) collective-permute-start(f32[256,256]{1,0:T(8,128)S(1)} %select_select_fusion), channel_id=1, source_target_pairs={{0,2},{2,0},{3,1},{4,6},{6,4},{7,5},{16,18},{18,16},{19,17},{20,22... | collective-permute-start | bytes 786440 | tf_op jit(solution)/shard_map/ppermute | solution.py:306
  9.2 30.4 %collective-permute-start.5 = (f32[256,256]{1,0:T(8,128)S(1)}, f32[256,256]{1,0:T(8,128)S(1)}, u32[]{:S(2)}, u32[]{:S(2)}) collective-permute-start(f32[256,256]{1,0:T(8,128)S(1)} %select_select_fusion), channel_id=1, source_target_pairs={{0,10},{2,8},{3,9},{4,14},{6,12},{7,13},{16,26},{18,24},{19,25},{2... | collective-permute-start | bytes 786440 | tf_op jit(solution)/shard_map/ppermute | solution.py:306
  22.6 17.8 %collective-permute-start.7 = (f32[256,256]{1,0:T(8,128)S(1)}, f32[256,256]{1,0:T(8,128)S(1)}, u32[]{:S(2)}, u32[]{:S(2)}) collective-permute-start(f32[256,256]{1,0:T(8,128)S(1)} %broadcast_select_fusion), channel_id=1, source_target_pairs={{4,6},{7,5},{8,10},{11,9},{12,14},{15,13},{20,22},{23,21},{24,26},... | collective-permute-start | bytes 786440 | tf_op jit(solution)/shard_map/ppermute | solution.py:306
  25.6 17.2 %collective-permute-start.8 = (f32[256,256]{1,0:T(8,128)S(1)}, f32[256,256]{1,0:T(8,128)S(1)}, u32[]{:S(2)}, u32[]{:S(2)}) collective-permute-start(f32[256,256]{1,0:T(8,128)S(1)} %broadcast_select_fusion), channel_id=1, source_target_pairs={{5,6},{6,5},{9,10},{10,9},{13,14},{14,13},{21,22},{22,21},{25,26},... | collective-permute-start | bytes 786440 | tf_op jit(solution)/shard_map/ppermute | solution.py:306
  39.8 3.3 %collective-permute-start.9 = (f32[2,256,256]{2,1,0:T(8,128)S(1)}, f32[2,256,256]{2,1,0:T(8,128)S(1)}, u32[]{:S(2)}, u32[]{:S(2)}) collective-permute-start(f32[2,256,256]{2,1,0:T(8,128)S(1)} %pad_maximum_fusion.own_ref), channel_id=1, source_target_pairs={{0,1},{1,0},{2,3},{3,2},{4,5},{5,4},{6,7},{7,6},{8,9},{9,8},{10,11... | collective-permute-start | bytes 1572872 | tf_op jit(solution)/shard_map/ppermute | solution.py:306
  42.9 11.9 %collective-permute-start.11 = (f32[2,256,256]{2,1,0:T(8,128)S(1)}, f32[2,256,256]{2,1,0:T(8,128)S(1)}, u32[]{:S(2)}, u32[]{:S(2)}) collective-permute-start(f32[2,256,256]{2,1,0:T(8,128)S(1)} %pad_maximum_fusion.1.at_ref), channel_id=1, source_target_pairs={{0,4},{1,9},{2,6},{3,11},{4,0},{5,13},{6,2},{7,15},{8,12},{9,1},{1... | collective-permute-start | bytes 1572872 | tf_op jit(solution)/shard_map/ppermute | solution.py:306
  43.0 11.9 %collective-permute-start.12 = (f32[2,256,256]{2,1,0:T(8,128)S(1)}, f32[2,256,256]{2,1,0:T(8,128)S(1)}, u32[]{:S(2)}, u32[]{:S(2)}) collective-permute-start(f32[2,256,256]{2,1,0:T(8,128)S(1)} %pad_maximum_fusion.1.at_ref), channel_id=1, source_target_pairs={{0,8},{1,5},{2,10},{3,7},{4,12},{5,1},{6,14},{7,3},{8,0},{9,13},{1... | collective-permute-start | bytes 1572872 | tf_op jit(solution)/shard_map/ppermute | solution.py:306
  50.9 4.0 %collective-permute-start.10 = (f32[2,256,256]{2,1,0:T(8,128)S(1)}, f32[2,256,256]{2,1,0:T(8,128)S(1)}, u32[]{:S(2)}, u32[]{:S(2)}) collective-permute-start(f32[2,256,256]{2,1,0:T(8,128)S(1)} %pad_maximum_fusion.2.own_ref), channel_id=1, source_target_pairs={{0,1},{1,0},{2,3},{3,2},{4,5},{5,4},{6,7},{7,6},{8,9},{9,8},{10,11... | collective-permute-start | bytes 1572872 | tf_op jit(solution)/shard_map/ppermute | solution.py:306
  54.9 8.0 %collective-permute-start.13 = (f32[2,256,256]{2,1,0:T(8,128)S(1)}, f32[2,256,256]{2,1,0:T(8,128)S(1)}, u32[]{:S(2)}, u32[]{:S(2)}) collective-permute-start(f32[2,256,256]{2,1,0:T(8,128)S(1)} %collective-permute-done.11.a_ref), channel_id=1, source_target_pairs={{0,8},{1,5},{2,10},{3,7},{4,12},{5,1},{6,14},{7,3},{8,0},{9,13},{1... | collective-permute-start | bytes 1572872 | tf_op jit(solution)/shard_map/ppermute | solution.py:306
  54.9 8.0 %copy-start = (f32[2,1,4,1,256,256]{5,4,3,2,1,0:T(8,128)S(1)}, f32[2,1,4,1,256,256]{5,4,3,2,1,0:T(8,128)}, u32[]{:S(2)}) copy-start(f32[2,1,4,1,256,256]{5,4,3,2,1,0:T(8,128)} %param.2) | copy-start | bytes 6291460
